TPU v7x, 256 devices: a whole 4x4x8 slice. The times are simulated.
256 devices in a mesh: band: 4 (over x_lo, core), grid: 64 (over z, x_hi, y).
Axes of the slice: x: 4 (x_hi: 2, x_lo: 2; x = x_hi * 2 + x_lo), y: 4, z: 8, core: 2. Of those that a mesh axis runs over, the one named last changes fastest.
Arguments:
- states: float32 [64, 512, 8, 128], P('band', 'grid'), may hold values from -6 to 6
- potential: float32 [512, 8, 128], P('grid'), may hold values from -1 to 1
- proj_index: int32 [128, 128], replicated, may hold values from 0 to 524287, as said below
- proj_value: float32 [128, 128], replicated, may hold values from 0 to 1
- proj_strength: float32 [128], replicated, may hold values from 0.5 to 4
Outputs:
- filtered: float32 [64, 512, 8, 128], P('band', 'grid')
- gram: float32 [64, 64], P('band')
- hamiltonian: float32 [64, 64], P('band')
Inputs may be any that keep to these rules, and one draw needn't show every extreme that they name: `proj_index`: along the first grid dimension every support point lies within 8 planes of its atom's centre plane.
All inputs are finite; a program needn't handle non-finite values.
Results may differ from a plain program's by a relative error of at most 0.0001.
Values sent between devices are 32-bit elements; how exact they have to be, the bound alone decides.
No kernel may reach another device: no remote copies, remote signals or barrier semaphores. Data moves between devices by JAX's collectives and lax.ppermute only.
A program may use at most 64 MiB of HBM per device.

v0:
```python
import functools

import jax
import jax.numpy as jnp
from jax import lax
from jax.experimental import pallas as pl
from jax.experimental.pallas import tpu as pltpu
from jax.sharding import PartitionSpec as P

RADIUS = 4
DEGREE = 4
WINDOW = 17

stencil_weights = (-205.0 / 72.0, 1.6, -0.2, 8.0 / 315.0, -1.0 / 560.0)
filter_centre = 10.0
filter_half = 6.0

VMEM = pl.BlockSpec(memory_space=pltpu.VMEM)
SMEM = pl.BlockSpec(memory_space=pltpu.SMEM)
NT = (((1,), (1,)), ((), ()))


def call(kernel, name, out_shape, in_specs, out_specs, scratch=(), flops=4_000_000, nbytes=4_000_000):
    return pl.pallas_call(
        kernel,
        name=name,
        out_shape=out_shape,
        in_specs=in_specs,
        out_specs=out_specs,
        scratch_shapes=list(scratch),
        compiler_params=pltpu.CompilerParams(vmem_limit_bytes=20 << 20),
        cost_estimate=pl.CostEstimate(flops=flops, bytes_accessed=nbytes, transcendentals=0),
    )


def build_kernel(planes, info, idx, val, blocks, table):
    base = info[0] * planes
    atoms, points = idx.shape
    cells = 8 * 128
    table[2, 0] = 0
    table[2, 1] = info[0]

    def pick(a, carry):
        low = info[8 + a]
        high = info[8 + atoms + a]

        @pl.when((high >= base) & (low < base + planes))
        def _():
            n = table[2, 0]
            table[0, n] = a
            table[1, n] = jnp.clip(low - base, 0, planes - WINDOW)
            table[2, 0] = n + 1

        return carry

    lax.fori_loop(0, atoms, pick, 0)

    def build(n, carry):
        a = table[0, n]
        rel = idx[pl.ds(a, 1), :] - (base + table[1, n]) * cells
        inside = (rel >= 0) & (rel < WINDOW * cells)
        w = jnp.where(inside, val[pl.ds(a, 1), :], 0.0)
        row = rel >> 7
        col = rel & 127
        hit = lax.broadcasted_iota(jnp.int32, (WINDOW * 8, points), 0) == row
        cols = (lax.broadcasted_iota(jnp.int32, (128, points), 0) == col).astype(jnp.float32).astype(jnp.bfloat16)
        w1 = w.astype(jnp.bfloat16).astype(jnp.float32)
        w2 = (w - w1).astype(jnp.bfloat16).astype(jnp.float32)
        w3 = w - w1 - w2
        total = None
        for part in (w3, w2, w1):
            rows = jnp.where(hit, part, 0.0).astype(jnp.bfloat16)
            term = lax.dot_general(rows, cols, NT, preferred_element_type=jnp.float32)
            total = term if total is None else total + term
        blocks[pl.ds(n, 1)] = total.reshape(1, WINDOW, 8, 128)
        return carry

    lax.fori_loop(0, table[2, 0], build, 0)


def coefficients(table, field, blocks, sums):
    sums[...] = jnp.zeros_like(sums)

    def one(n, carry):
        a = table[0, n]
        st = table[1, n]
        acc = [None, None]
        for i in range(WINDOW):
            b = blocks[n, i]
            for s in range(2):
                t = b * field(s, st + i)
                acc[s] = t if acc[s] is None else acc[s] + t
        for s in range(2):
            sums[s, pl.ds(a, 1), :] = jnp.sum(acc[s], axis=0, keepdims=True)
        return carry

    lax.fori_loop(0, table[2, 0], one, 0)
    ones = jnp.ones((8, 128), jnp.float32)
    return [
        lax.dot_general(ones, sums[s], NT, precision=lax.Precision.HIGHEST, preferred_element_type=jnp.float32)
        for s in range(2)
    ]


def first_kernel(table, y, blocks, up, down, sums):
    slabs = y.shape[0]
    parts = coefficients(table, lambda s, p: y[p >> 3, s, p & 7], blocks, sums)
    for s in range(2):
        up[s, 0:4] = y[slabs - 1, s, 4:8]
        down[s, 0:4] = y[0, s, 0:4]
        up[s, 4] = parts[s]
        down[s, 4] = parts[s]


def lane_weights():
    lane = lax.broadcasted_iota(jnp.int32, (8, 128), 1)
    out = []
    for k in range(1, RADIUS + 1):
        c = stencil_weights[k]
        out.append((k, jnp.where(lane >= k, c, 0.0)))
        out.append((128 - k, jnp.where(lane < 128 - k, c, 0.0)))
    return out


def row_weights():
    row = lax.broadcasted_iota(jnp.int32, (8, 128), 0)
    out = []
    for r in range(1, 8):
        near = stencil_weights[r] if r <= RADIUS else 0.0
        far = stencil_weights[8 - r] if 8 - r <= RADIUS else 0.0
        out.append((r, jnp.where(row >= r, near, far)))
    return out


def step_kernel(mode, table, y, *refs):
    has_prev = mode in ("middle", "last")
    refs = list(refs)
    prev = refs.pop(0) if has_prev else None
    v, blocks, strength, below, above, own = refs[:6]
    refs = refs[6:]
    if mode == "image":
        (send, pad, new, splat) = refs
        alpha, sigma = 1.0, 0.0
    else:
        (out, up, down, pad, new, splat, sums) = refs
        alpha = (1.0 if mode == "first" else 2.0) / filter_half
        sigma = filter_centre
    slabs = y.shape[0]
    planes = slabs * 8
    z = table[2, 1]
    has_low = z > 0
    has_high = z < lax.axis_size("grid") // slabs - 1
    for s in range(2):
        pad[s, 0:4] = jnp.where(has_low, below[s, 0:4], 0.0)
        pad[s, planes + 4 : planes + 8] = jnp.where(has_high, above[s, 0:4], 0.0)
        for j in range(slabs):
            pad[s, 4 + 8 * j : 12 + 8 * j] = y[j, s]
    half = -0.5 * alpha
    lanes = [(k, w * half) for k, w in lane_weights()]
    rows = [(k, w * half) for k, w in row_weights()]
    centre = half * 3.0 * stencil_weights[0] - alpha * sigma

    def block(j, carry):
        for s in range(2):
            line = [pad[s, 8 * j + t] for t in range(16)]
            for t in range(8):
                mid = line[t + 4]
                acc = (alpha * v[j, 2, t] + centre) * mid
                for k in range(1, RADIUS + 1):
                    acc = acc + (half * stencil_weights[k]) * (line[t + 4 + k] + line[t + 4 - k])
                for k, w in rows:
                    acc = acc + w * pltpu.roll(mid, k, 0)
                for k, w in lanes:
                    acc = acc + w * pltpu.roll(mid, k, 1)
                if has_prev:
                    acc = acc - prev[j, s, t]
                new[s, 8 * j + t] = acc
        return carry

    lax.fori_loop(0, slabs, block, 0)

    for s in range(2):
        total = (own[s, 4] + below[s, 4] + above[s, 4]) * strength[...] * alpha
        splat[s] = jnp.transpose(jnp.broadcast_to(total[0:1], (128, 128)))

    def spread(n, carry):
        a = table[0, n]
        st = table[1, n]
        c = [jnp.broadcast_to(splat[s, pl.ds(a, 1), :], (8, 128)) for s in range(2)]
        for i in range(WINDOW):
            b = blocks[n, i]
            for s in range(2):
                new[s, st + i] = new[s, st + i] + c[s] * b
        return carry

    lax.fori_loop(0, table[2, 0], spread, 0)

    if mode == "image":
        for s in range(2):
            for j in range(slabs):
                for t in range(8):
                    d = (t // 2) * slabs + j
                    q = 8 * (t % 2)
                    send[d, s, 0, q : q + 8] = y[j, s, t]
                    send[d, s, 1, q : q + 8] = new[s, 8 * j + t]
    else:
        parts = coefficients(table, lambda s, p: new[s, p], blocks, sums)
        for s in range(2):
            for j in range(slabs):
                out[j, s] = new[s, 8 * j : 8 * j + 8]
            up[s, 0:4] = new[s, planes - 4 : planes]
            down[s, 0:4] = new[s, 0:4]
            up[s, 4] = parts[s]
            down[s, 4] = parts[s]


def product_kernel(states, got, out):
    total = None
    for r in range(16):
        f = got[pl.ds(r, states, stride=32), :]
        h = got[pl.ds(16 + r, states, stride=32), :]
        term = lax.dot_general(
            jnp.concatenate([f, h], axis=0), f, NT, precision=lax.Precision.HIGHEST, preferred_element_type=jnp.float32
        )
        total = term if total is None else total + term
    out[...] = jnp.concatenate([total[0:states], total[states : 2 * states]], axis=1)


def per_device(states, potential, proj_index, proj_value, proj_strength):
    f32 = jnp.float32
    count, depth, ny, nz = states.shape
    atoms = proj_index.shape[0]
    grid = lax.axis_size("grid")
    bands = lax.axis_size("band")
    group = 8
    zs = grid // group
    per = count // group
    planes = group * depth
    in_plane = [[z * group + j for j in range(group)] for z in range(zs)]
    along_z = [[z * group + j for z in range(zs)] for j in range(group)]
    whole_plane = [[b * grid + z * group + j for b in range(bands) for j in range(group)] for z in range(zs)]

    z = lax.axis_index("grid") // group
    support = proj_index >> 10
    info = jnp.concatenate(
        [jnp.full((8,), z, jnp.int32), jnp.min(support, axis=1), jnp.max(support, axis=1)]
    ).astype(jnp.int32)
    blocks, table = call(
        functools.partial(build_kernel, planes),
        "build",
        (jax.ShapeDtypeStruct((atoms, WINDOW, ny, nz), f32), jax.ShapeDtypeStruct((3, 128), jnp.int32)),
        [SMEM, VMEM, VMEM],
        (VMEM, SMEM),
    )(info, proj_index, proj_value)

    parcel = jnp.concatenate(
        [
            states.reshape(group, per, depth, ny, nz),
            jnp.broadcast_to(potential, (group, 1, depth, ny, nz)),
        ],
        axis=1,
    )
    start = lax.all_to_all(parcel, "grid", 0, 0, axis_index_groups=in_plane, tiled=True)

    field = jax.ShapeDtypeStruct((group, per, depth, ny, nz), f32)
    message = jax.ShapeDtypeStruct((per, 5, ny, nz), f32)
    sums = pltpu.VMEM((per, atoms, 128), f32)
    pad = pltpu.VMEM((per, planes + 8, ny, nz), f32)
    new = pltpu.VMEM((per, planes, ny, nz), f32)
    strength = proj_strength.reshape(1, atoms)

    up, down = call(first_kernel, "first", (message, message), [SMEM, VMEM, VMEM], (VMEM, VMEM), [sums])(
        table, start, blocks
    )

    def exchange(up, down):
        below = lax.ppermute(up, "grid", [(i, (i + group) % grid) for i in range(grid)])
        above = lax.ppermute(down, "grid", [(i, (i - group) % grid) for i in range(grid)])
        return below, above

    previous, current = None, start
    for k in range(DEGREE):
        mode = "first" if k == 0 else ("last" if k == DEGREE - 1 else "middle")
        below, above = exchange(up, down)
        args = [table, current] + ([previous] if k else []) + [start, blocks, strength, below, above, up]
        following, up, down = call(
            functools.partial(step_kernel, mode),
            "step",
            (field, message, message),
            [SMEM] + [VMEM] * (len(args) - 1),
            (VMEM,) * 3,
            [pad, new, sums, sums],
        )(*args)
        previous, current = current, following

    below, above = exchange(up, down)
    filtered = lax.all_to_all(current, "grid", 0, 0, axis_index_groups=in_plane, tiled=True).reshape(states.shape)
    send = call(
        functools.partial(step_kernel, "image"),
        "image",
        jax.ShapeDtypeStruct((bands * group, per, 2, 2 * ny, nz), f32),
        [SMEM] + [VMEM] * 7,
        VMEM,
        [pad, new, sums],
    )(table, current, start, blocks, strength, below, above, up)
    got = lax.all_to_all(send, ("band", "grid"), 0, 0, axis_index_groups=whole_plane, tiled=True)
    everyone = bands * count
    part = call(
        functools.partial(product_kernel, everyone),
        "product",
        jax.ShapeDtypeStruct((everyone, 2 * everyone), f32),
        [VMEM],
        VMEM,
    )(got.reshape(everyone * 32, nz))

    rows = lax.all_to_all(part.reshape(bands, count, 2 * everyone), "band", 0, 0, tiled=True).sum(axis=0)
    for members in (in_plane, along_z):
        copies = jnp.broadcast_to(rows, (group, *rows.shape))
        rows = lax.all_to_all(copies, "grid", 0, 0, axis_index_groups=members, tiled=True).sum(axis=0)
    rows = rows / float(grid * depth * ny * nz)
    return filtered, rows[:, :everyone], rows[:, everyone:]


def solution(mesh):
    in_specs = (P("band", "grid", None, None), P("grid", None, None), P(), P(), P())
    out_specs = (P("band", "grid", None, None), P("band", None), P("band", None))
    return jax.shard_map(
        per_device, mesh=mesh, in_specs=in_specs, out_specs=out_specs, check_vma=False
    )
```

profile of v0, /device:TPU:2, one launch (start us, length us, event | category | flops | bytes accessed | tf_op | source)
XLA Modules:
  0.0 150.1 jit_solution(6720374851719397179)
XLA Ops:
  1.4 2.0 %pad_maximum_fusion = f32[8,3,8,8,128]{4,3,2,1,0:T(8,128)} fusion(f32[8,1,8,8,128]{4,3,2,1,0:T(8,128)S(1)} %broadcast_in_dim.13, f32[8,2,8,8,128]{4,3,2,1,0:T(8,128)} %bitcast.13), kind=kLoop, calls=%fused_computation | loop fusion | flops 196608 | bytes 1572864 | tf_op jit(solution)/shard_map/concatenate | solution.py:256
  3.4 6.0 %all-to-all-start = ((f32[8,3,8,8,128]{4,3,2,1,0:T(8,128)}), f32[8,3,8,8,128]{4,3,2,1,0:T(8,128)S(1)}, u32[]{:S(2)}, u32[]{:S(2)}) async-start(f32[8,3,8,8,128]{4,3,2,1,0:T(8,128)} %pad_maximum_fusion), calls=%async_computation | async-start | bytes 1572864 | tf_op jit(solution)/shard_map/all_to_all | solution.py:263
  12.2 6.0 %build.1 = (f32[128,17,8,128]{3,2,1,0:T(8,128)S(1)}, s32[3,128]{1,0:T(4,128)S(1)}) custom-call(s32[264]{0:T(512)S(1)} %pad_add_fusion.info, s32[128,128]{1,0:T(8,128)S(1)} %copy-done.2, f32[128,128]{1,0:T(8,128)S(1)} %copy-done.3), custom_call_target="tpu_custom_call" | custom-call | flops 4000000 | bytes 4000000 | tf_op jit(solution)/shard_map/build/pallas_call | solution.py:248
  18.2 3.4 %copy-done = f32[128,17,8,128]{3,2,1,0:T(8,128)} copy-done((f32[128,17,8,128]{3,2,1,0:T(8,128)}, f32[128,17,8,128]{3,2,1,0:T(8,128)S(1)}, u32[]{:S(2)}) %copy-start) | copy-done | bytes 8912920
  21.6 1.2 all-to-all-done.y.refs_0_.refs_1_
  22.9 3.5 %copy-done.1 = f32[128,17,8,128]{3,2,1,0:T(8,128)S(1)} copy-done((f32[128,17,8,128]{3,2,1,0:T(8,128)S(1)}, f32[128,17,8,128]{3,2,1,0:T(8,128)}, u32[]{:S(2)}) %copy-start.1) | copy-done | bytes 8912920
  26.4 1.5 %first.1 = (f32[2,5,8,128]{3,2,1,0:T(8,128)S(1)}, f32[2,5,8,128]{3,2,1,0:T(8,128)S(1)}) custom-call(s32[3,128]{1,0:T(4,128)S(1)} %get-tuple-element.19.table, f32[8,3,8,8,128]{4,3,2,1,0:T(8,128)S(1)} %all-to-all-done.y.refs_0_.refs_1_, f32[128,17,8,128]{3,2,1,0:T(8,128)S(1)} %copy-done.1), custom_call_target="tpu_custom_call" | custom-call | flops 4000000 | bytes 4000000 | tf_op jit(solution)/shard_map/first/pallas_call | solution.py:272
  27.9 2.0 %collective-permute-start = (f32[2,5,8,128]{3,2,1,0:T(8,128)S(1)}, f32[2,5,8,128]{3,2,1,0:T(8,128)S(1)}, u32[]{:S(2)}, u32[]{:S(2)}) collective-permute-start(f32[2,5,8,128]{3,2,1,0:T(8,128)S(1)} %get-tuple-element.21.refs_5_), channel_id=1, source_target_pairs={{0,8},{1,9},{2,10},{3,11},{4,12},{5,13},{6,14},{7,15},{8,16},{9,17... | collective-permute-start | bytes 122888 | tf_op jit(solution)/shard_map/ppermute | solution.py:277
  30.0 4.1 %collective-permute-start.1 = (f32[2,5,8,128]{3,2,1,0:T(8,128)S(1)}, f32[2,5,8,128]{3,2,1,0:T(8,128)S(1)}, u32[]{:S(2)}, u32[]{:S(2)}) collective-permute-start(f32[2,5,8,128]{3,2,1,0:T(8,128)S(1)} %get-tuple-element.22), channel_id=1, source_target_pairs={{0,56},{1,57},{2,58},{3,59},{4,60},{5,61},{6,62},{7,63},{8,0},{9,1... | collective-permute-start | bytes 122888 | tf_op jit(solution)/shard_map/ppermute | solution.py:278
  34.1 1.9 %collective-permute-done.refs_3_ = f32[2,5,8,128]{3,2,1,0:T(8,128)S(1)} collective-permute-done((f32[2,5,8,128]{3,2,1,0:T(8,128)S(1)}, f32[2,5,8,128]{3,2,1,0:T(8,128)S(1)}, u32[]{:S(2)}, u32[]{:S(2)}) %collective-permute-start) | collective-permute-done | bytes 40992 | tf_op jit(solution)/shard_map/ppermute | solution.py:277
  36.0 3.3 %step.4 = (f32[8,2,8,8,128]{4,3,2,1,0:T(8,128)S(1)}, f32[2,5,8,128]{3,2,1,0:T(8,128)S(1)}, f32[2,5,8,128]{3,2,1,0:T(8,128)S(1)}) custom-call(s32[3,128]{1,0:T(4,128)S(1)} %get-tuple-element.19.table, f32[8,3,8,8,128]{4,3,2,1,0:T(8,128)S(1)} %all-to-all-done.y.refs_0_.refs_1_, f32[8,3,8,8,128]{4,3,2,1,0:T(8,128)S(1)} %all-to-all-done.y.refs_0_.refs_1_, ...), custom_call_target="tpu_custom_call" | custom-call | flops 4000000 | bytes 4000000 | tf_op jit(solution)/shard_map/step/pallas_call | solution.py:286
  39.8 3.1 %collective-permute-start.3 = (f32[2,5,8,128]{3,2,1,0:T(8,128)S(1)}, f32[2,5,8,128]{3,2,1,0:T(8,128)S(1)}, u32[]{:S(2)}, u32[]{:S(2)}) collective-permute-start(f32[2,5,8,128]{3,2,1,0:T(8,128)S(1)} %get-tuple-element.25), channel_id=1, source_target_pairs={{0,56},{1,57},{2,58},{3,59},{4,60},{5,61},{6,62},{7,63},{8,0},{9,1... | collective-permute-start | bytes 122888 | tf_op jit(solution)/shard_map/ppermute | solution.py:278
  42.9 1.9 %collective-permute-done.2.refs_4_ = f32[2,5,8,128]{3,2,1,0:T(8,128)S(1)} collective-permute-done((f32[2,5,8,128]{3,2,1,0:T(8,128)S(1)}, f32[2,5,8,128]{3,2,1,0:T(8,128)S(1)}, u32[]{:S(2)}, u32[]{:S(2)}) %collective-permute-start.2) | collective-permute-done | bytes 40992 | tf_op jit(solution)/shard_map/ppermute | solution.py:277
  44.9 3.3 %step.5 = (f32[8,2,8,8,128]{4,3,2,1,0:T(8,128)S(1)}, f32[2,5,8,128]{3,2,1,0:T(8,128)S(1)}, f32[2,5,8,128]{3,2,1,0:T(8,128)S(1)}) custom-call(s32[3,128]{1,0:T(4,128)S(1)} %get-tuple-element.19.table, f32[8,2,8,8,128]{4,3,2,1,0:T(8,128)S(1)} %get-tuple-element.23.y.refs_0_, f32[8,3,8,8,128]{4,3,2,1,0:T(8,128)S(1)} %all-to-all-done.y.refs_0_.refs_1_, ...), custom_call_target="tpu_custom_call" | custom-call | flops 4000000 | bytes 4000000 | tf_op jit(solution)/shard_map/step/pallas_call | solution.py:286
  48.2 3.4 %collective-permute-start.4 = (f32[2,5,8,128]{3,2,1,0:T(8,128)S(1)}, f32[2,5,8,128]{3,2,1,0:T(8,128)S(1)}, u32[]{:S(2)}, u32[]{:S(2)}) collective-permute-start(f32[2,5,8,128]{3,2,1,0:T(8,128)S(1)} %get-tuple-element.27.refs_6_), channel_id=1, source_target_pairs={{0,8},{1,9},{2,10},{3,11},{4,12},{5,13},{6,14},{7,15},{8,16},{9,17... | collective-permute-start | bytes 122888 | tf_op jit(solution)/shard_map/ppermute | solution.py:277
  51.8 1.9 %collective-permute-done.4.refs_4_ = f32[2,5,8,128]{3,2,1,0:T(8,128)S(1)} collective-permute-done((f32[2,5,8,128]{3,2,1,0:T(8,128)S(1)}, f32[2,5,8,128]{3,2,1,0:T(8,128)S(1)}, u32[]{:S(2)}, u32[]{:S(2)}) %collective-permute-start.4) | collective-permute-done | bytes 40992 | tf_op jit(solution)/shard_map/ppermute | solution.py:277
  53.7 1.9 %collective-permute-done.5.refs_5_ = f32[2,5,8,128]{3,2,1,0:T(8,128)S(1)} collective-permute-done((f32[2,5,8,128]{3,2,1,0:T(8,128)S(1)}, f32[2,5,8,128]{3,2,1,0:T(8,128)S(1)}, u32[]{:S(2)}, u32[]{:S(2)}) %collective-permute-start.5) | collective-permute-done | bytes 40992 | tf_op jit(solution)/shard_map/ppermute | solution.py:278
  55.5 3.3 %step.6 = (f32[8,2,8,8,128]{4,3,2,1,0:T(8,128)S(1)}, f32[2,5,8,128]{3,2,1,0:T(8,128)S(1)}, f32[2,5,8,128]{3,2,1,0:T(8,128)S(1)}) custom-call(s32[3,128]{1,0:T(4,128)S(1)} %get-tuple-element.19.table, f32[8,2,8,8,128]{4,3,2,1,0:T(8,128)S(1)} %get-tuple-element.26.y.refs_0_, f32[8,2,8,8,128]{4,3,2,1,0:T(8,128)S(1)} %get-tuple-element.23.y.refs_0_, ...), custom_call_target="tpu_custom_call" | custom-call | flops 4000000 | bytes 4000000 | tf_op jit(solution)/shard_map/step/pallas_call | solution.py:286
  58.9 2.4 %collective-permute-start.6 = (f32[2,5,8,128]{3,2,1,0:T(8,128)S(1)}, f32[2,5,8,128]{3,2,1,0:T(8,128)S(1)}, u32[]{:S(2)}, u32[]{:S(2)}) collective-permute-start(f32[2,5,8,128]{3,2,1,0:T(8,128)S(1)} %get-tuple-element.30.refs_6_), channel_id=1, source_target_pairs={{0,8},{1,9},{2,10},{3,11},{4,12},{5,13},{6,14},{7,15},{8,16},{9,17... | collective-permute-start | bytes 122888 | tf_op jit(solution)/shard_map/ppermute | solution.py:277
  62.1 2.0 %collective-permute-done.6.refs_4_ = f32[2,5,8,128]{3,2,1,0:T(8,128)S(1)} collective-permute-done((f32[2,5,8,128]{3,2,1,0:T(8,128)S(1)}, f32[2,5,8,128]{3,2,1,0:T(8,128)S(1)}, u32[]{:S(2)}, u32[]{:S(2)}) %collective-permute-start.6) | collective-permute-done | bytes 40992 | tf_op jit(solution)/shard_map/ppermute | solution.py:277
  65.3 4.0 %step.7 = (f32[8,2,8,8,128]{4,3,2,1,0:T(8,128)}, f32[2,5,8,128]{3,2,1,0:T(8,128)S(1)}, f32[2,5,8,128]{3,2,1,0:T(8,128)S(1)}) custom-call(s32[3,128]{1,0:T(4,128)S(1)} %get-tuple-element.19.table, f32[8,2,8,8,128]{4,3,2,1,0:T(8,128)S(1)} %get-tuple-element.29.y, f32[8,2,8,8,128]{4,3,2,1,0:T(8,128)S(1)} %get-tuple-element.26.y.refs_0_, ...), custom_call_target="tpu_custom_call" | custom-call | flops 4000000 | bytes 4000000 | tf_op jit(solution)/shard_map/step/pallas_call | solution.py:286
  69.3 2.3 %collective-permute-start.8 = (f32[2,5,8,128]{3,2,1,0:T(8,128)S(1)}, f32[2,5,8,128]{3,2,1,0:T(8,128)S(1)}, u32[]{:S(2)}, u32[]{:S(2)}) collective-permute-start(f32[2,5,8,128]{3,2,1,0:T(8,128)S(1)} %get-tuple-element.33.refs_5_), channel_id=1, source_target_pairs={{0,8},{1,9},{2,10},{3,11},{4,12},{5,13},{6,14},{7,15},{8,16},{9,17... | collective-permute-start | bytes 122888 | tf_op jit(solution)/shard_map/ppermute | solution.py:277
  72.5 2.0 %collective-permute-done.8.refs_3_ = f32[2,5,8,128]{3,2,1,0:T(8,128)S(1)} collective-permute-done((f32[2,5,8,128]{3,2,1,0:T(8,128)S(1)}, f32[2,5,8,128]{3,2,1,0:T(8,128)S(1)}, u32[]{:S(2)}, u32[]{:S(2)}) %collective-permute-start.8) | collective-permute-done | bytes 40992 | tf_op jit(solution)/shard_map/ppermute | solution.py:277
  75.6 3.1 %image.1 = f32[32,2,2,16,128]{4,3,2,1,0:T(8,128)S(1)} custom-call(s32[3,128]{1,0:T(4,128)S(1)} %get-tuple-element.19.table, f32[8,2,8,8,128]{4,3,2,1,0:T(8,128)} %get-tuple-element.32.y, f32[8,3,8,8,128]{4,3,2,1,0:T(8,128)S(1)} %all-to-all-done.y.refs_0_.refs_1_, f32[128,17,8,128]{3,2,1,0:T(8,128)S(1)} %copy-done.1, f32[1,128]{1,0:T(1,128)S(1)} %bitcast.11, ...), custom_call_target="tpu_custom_call" | custom-call | flops 4000000 | bytes 4000000 | tf_op jit(solution)/shard_map/image/pallas_call | solution.py:298
  78.8 24.6 %all_to_all.30 = f32[32,2,2,16,128]{4,3,2,1,0:T(8,128)S(1)} all-to-all(f32[32,2,2,16,128]{4,3,2,1,0:T(8,128)S(1)} %image.1), channel_id=1, replica_groups={{0,1,2,3,4,5,6,7,64,65,66,67,68,69,70,71,128,129,130,131,132,133,134,13..., dimensions={0} | all-to-all | bytes 2097152 | tf_op jit(solution)/shard_map/all_to_all | solution.py:306
  103.3 1.2 product.1
  104.5 5.7 %all_to_all.31 = f32[4,16,128]{2,1,0:T(8,128)S(1)} all-to-all(f32[4,16,128]{2,1,0:T(8,128)S(1)} %bitcast.6), channel_id=1, replica_groups=mesh['band'=4,'grid'=64] {'band'}, dimensions={0} | all-to-all | bytes 65536 | tf_op jit(solution)/shard_map/all_to_all | solution.py:316
  110.3 10.8 %all_to_all.32 = f32[8,16,128]{2,1,0:T(8,128)S(1)} all-to-all(f32[8,16,128]{2,1,0:T(8,128)S(1)} %broadcast_in_dim.14), channel_id=1, replica_groups={{0,1,2,3,4,5,6,7},{8,9,10,11,12,13,14,15},{16,17,18,19,20,21,22,23},{24..., dimensions={0} | all-to-all | bytes 131072 | tf_op jit(solution)/shard_map/all_to_all | solution.py:319
  121.1 3.5 %all-to-all-start.1 = ((f32[8,2,8,8,128]{4,3,2,1,0:T(8,128)}), f32[8,2,8,8,128]{4,3,2,1,0:T(8,128)S(1)}, u32[]{:S(2)}, u32[]{:S(2)}) async-start(f32[8,2,8,8,128]{4,3,2,1,0:T(8,128)} %get-tuple-element.32.y), calls=%async_computation.1 | async-start | bytes 1048576 | tf_op jit(solution)/shard_map/all_to_all | solution.py:297
  124.6 10.0 %all-to-all-done.1 = f32[8,2,8,8,128]{4,3,2,1,0:T(8,128)S(1)} async-done(((f32[8,2,8,8,128]{4,3,2,1,0:T(8,128)}), f32[8,2,8,8,128]{4,3,2,1,0:T(8,128)S(1)}, u32[]{:S(2)}, u32[]{:S(2)}) %all-to-all-start.1) | async-done | bytes 524320 | tf_op jit(solution)/shard_map/all_to_all | solution.py:297
  135.3 5.0 %all-to-all-start.5 = ((f32[8,16,128]{2,1,0:T(8,128)}), f32[8,16,128]{2,1,0:T(8,128)S(1)}, u32[]{:S(2)}, u32[]{:S(2)}) async-start(f32[8,16,128]{2,1,0:T(8,128)} %broadcast_in_dim.15), calls=%async_computation.5 | async-start | bytes 131072 | tf_op jit(solution)/shard_map/all_to_all | solution.py:319
  140.3 8.4 %all-to-all-done.5 = f32[8,16,128]{2,1,0:T(8,128)S(1)} async-done(((f32[8,16,128]{2,1,0:T(8,128)}), f32[8,16,128]{2,1,0:T(8,128)S(1)}, u32[]{:S(2)}, u32[]{:S(2)}) %all-to-all-start.5) | async-done | bytes 65568 | tf_op jit(solution)/shard_map/all_to_all | solution.py:319
  (28 shorter events, 10.4 us)
Async XLA Ops:
  0.6 35.4 %copy-start.4 = (f32[128]{0:T(128)S(1)}, f32[128]{0:T(128)}, u32[]{:S(2)}) copy-start(f32[128]{0:T(128)} %param.9) | copy-start | bytes 1540
  3.4 19.4 %all-to-all-start = ((f32[8,3,8,8,128]{4,3,2,1,0:T(8,128)}), f32[8,3,8,8,128]{4,3,2,1,0:T(8,128)S(1)}, u32[]{:S(2)}, u32[]{:S(2)}) async-start(f32[8,3,8,8,128]{4,3,2,1,0:T(8,128)} %pad_maximum_fusion), calls=%async_computation | async-start | bytes 1572864 | tf_op jit(solution)/shard_map/all_to_all | solution.py:263
  10.5 0.8 copy-start.2
  11.4 0.8 copy-start.3
  18.2 3.4 %copy-start = (f32[128,17,8,128]{3,2,1,0:T(8,128)}, f32[128,17,8,128]{3,2,1,0:T(8,128)S(1)}, u32[]{:S(2)}) copy-start(f32[128,17,8,128]{3,2,1,0:T(8,128)S(1)} %get-tuple-element.20.blocks.refs_1_.refs_2_) | copy-start | bytes 26738692
  22.9 3.5 %copy-start.1 = (f32[128,17,8,128]{3,2,1,0:T(8,128)S(1)}, f32[128,17,8,128]{3,2,1,0:T(8,128)}, u32[]{:S(2)}) copy-start(f32[128,17,8,128]{3,2,1,0:T(8,128)} %copy-done) | copy-start | bytes 26738692
  27.9 8.1 %collective-permute-start = (f32[2,5,8,128]{3,2,1,0:T(8,128)S(1)}, f32[2,5,8,128]{3,2,1,0:T(8,128)S(1)}, u32[]{:S(2)}, u32[]{:S(2)}) collective-permute-start(f32[2,5,8,128]{3,2,1,0:T(8,128)S(1)} %get-tuple-element.21.refs_5_), channel_id=1, source_target_pairs={{0,8},{1,9},{2,10},{3,11},{4,12},{5,13},{6,14},{7,15},{8,16},{9,17... | collective-permute-start | bytes 122888 | tf_op jit(solution)/shard_map/ppermute | solution.py:277
  30.0 6.1 %collective-permute-start.1 = (f32[2,5,8,128]{3,2,1,0:T(8,128)S(1)}, f32[2,5,8,128]{3,2,1,0:T(8,128)S(1)}, u32[]{:S(2)}, u32[]{:S(2)}) collective-permute-start(f32[2,5,8,128]{3,2,1,0:T(8,128)S(1)} %get-tuple-element.22), channel_id=1, source_target_pairs={{0,56},{1,57},{2,58},{3,59},{4,60},{5,61},{6,62},{7,63},{8,0},{9,1... | collective-permute-start | bytes 122888 | tf_op jit(solution)/shard_map/ppermute | solution.py:278
  39.4 5.5 %collective-permute-start.2 = (f32[2,5,8,128]{3,2,1,0:T(8,128)S(1)}, f32[2,5,8,128]{3,2,1,0:T(8,128)S(1)}, u32[]{:S(2)}, u32[]{:S(2)}) collective-permute-start(f32[2,5,8,128]{3,2,1,0:T(8,128)S(1)} %get-tuple-element.24.refs_6_), channel_id=1, source_target_pairs={{0,8},{1,9},{2,10},{3,11},{4,12},{5,13},{6,14},{7,15},{8,16},{9,17... | collective-permute-start | bytes 122888 | tf_op jit(solution)/shard_map/ppermute | solution.py:277
  39.8 5.0 %collective-permute-start.3 = (f32[2,5,8,128]{3,2,1,0:T(8,128)S(1)}, f32[2,5,8,128]{3,2,1,0:T(8,128)S(1)}, u32[]{:S(2)}, u32[]{:S(2)}) collective-permute-start(f32[2,5,8,128]{3,2,1,0:T(8,128)S(1)} %get-tuple-element.25), channel_id=1, source_target_pairs={{0,56},{1,57},{2,58},{3,59},{4,60},{5,61},{6,62},{7,63},{8,0},{9,1... | collective-permute-start | bytes 122888 | tf_op jit(solution)/shard_map/ppermute | solution.py:278
  48.2 5.5 %collective-permute-start.4 = (f32[2,5,8,128]{3,2,1,0:T(8,128)S(1)}, f32[2,5,8,128]{3,2,1,0:T(8,128)S(1)}, u32[]{:S(2)}, u32[]{:S(2)}) collective-permute-start(f32[2,5,8,128]{3,2,1,0:T(8,128)S(1)} %get-tuple-element.27.refs_6_), channel_id=1, source_target_pairs={{0,8},{1,9},{2,10},{3,11},{4,12},{5,13},{6,14},{7,15},{8,16},{9,17... | collective-permute-start | bytes 122888 | tf_op jit(solution)/shard_map/ppermute | solution.py:277
  51.5 4.0 %collective-permute-start.5 = (f32[2,5,8,128]{3,2,1,0:T(8,128)S(1)}, f32[2,5,8,128]{3,2,1,0:T(8,128)S(1)}, u32[]{:S(2)}, u32[]{:S(2)}) collective-permute-start(f32[2,5,8,128]{3,2,1,0:T(8,128)S(1)} %get-tuple-element.28), channel_id=1, source_target_pairs={{0,56},{1,57},{2,58},{3,59},{4,60},{5,61},{6,62},{7,63},{8,0},{9,1... | collective-permute-start | bytes 122888 | tf_op jit(solution)/shard_map/ppermute | solution.py:278
  58.9 5.2 %collective-permute-start.6 = (f32[2,5,8,128]{3,2,1,0:T(8,128)S(1)}, f32[2,5,8,128]{3,2,1,0:T(8,128)S(1)}, u32[]{:S(2)}, u32[]{:S(2)}) collective-permute-start(f32[2,5,8,128]{3,2,1,0:T(8,128)S(1)} %get-tuple-element.30.refs_6_), channel_id=1, source_target_pairs={{0,8},{1,9},{2,10},{3,11},{4,12},{5,13},{6,14},{7,15},{8,16},{9,17... | collective-permute-start | bytes 122888 | tf_op jit(solution)/shard_map/ppermute | solution.py:277
  61.3 4.0 %collective-permute-start.7 = (f32[2,5,8,128]{3,2,1,0:T(8,128)S(1)}, f32[2,5,8,128]{3,2,1,0:T(8,128)S(1)}, u32[]{:S(2)}, u32[]{:S(2)}) collective-permute-start(f32[2,5,8,128]{3,2,1,0:T(8,128)S(1)} %get-tuple-element.31), channel_id=1, source_target_pairs={{0,56},{1,57},{2,58},{3,59},{4,60},{5,61},{6,62},{7,63},{8,0},{9,1... | collective-permute-start | bytes 122888 | tf_op jit(solution)/shard_map/ppermute | solution.py:278
  69.3 5.2 %collective-permute-start.8 = (f32[2,5,8,128]{3,2,1,0:T(8,128)S(1)}, f32[2,5,8,128]{3,2,1,0:T(8,128)S(1)}, u32[]{:S(2)}, u32[]{:S(2)}) collective-permute-start(f32[2,5,8,128]{3,2,1,0:T(8,128)S(1)} %get-tuple-element.33.refs_5_), channel_id=1, source_target_pairs={{0,8},{1,9},{2,10},{3,11},{4,12},{5,13},{6,14},{7,15},{8,16},{9,17... | collective-permute-start | bytes 122888 | tf_op jit(solution)/shard_map/ppermute | solution.py:277
  71.6 4.0 %collective-permute-start.9 = (f32[2,5,8,128]{3,2,1,0:T(8,128)S(1)}, f32[2,5,8,128]{3,2,1,0:T(8,128)S(1)}, u32[]{:S(2)}, u32[]{:S(2)}) collective-permute-start(f32[2,5,8,128]{3,2,1,0:T(8,128)S(1)} %get-tuple-element.34), channel_id=1, source_target_pairs={{0,56},{1,57},{2,58},{3,59},{4,60},{5,61},{6,62},{7,63},{8,0},{9,1... | collective-permute-start | bytes 122888 | tf_op jit(solution)/shard_map/ppermute | solution.py:278
  121.1 13.6 %all-to-all-start.1 = ((f32[8,2,8,8,128]{4,3,2,1,0:T(8,128)}), f32[8,2,8,8,128]{4,3,2,1,0:T(8,128)S(1)}, u32[]{:S(2)}, u32[]{:S(2)}) async-start(f32[8,2,8,8,128]{4,3,2,1,0:T(8,128)} %get-tuple-element.32.y), calls=%async_computation.1 | async-start | bytes 1048576 | tf_op jit(solution)/shard_map/all_to_all | solution.py:297
  135.3 13.4 %all-to-all-start.5 = ((f32[8,16,128]{2,1,0:T(8,128)}), f32[8,16,128]{2,1,0:T(8,128)S(1)}, u32[]{:S(2)}, u32[]{:S(2)}) async-start(f32[8,16,128]{2,1,0:T(8,128)} %broadcast_in_dim.15), calls=%async_computation.5 | async-start | bytes 131072 | tf_op jit(solution)/shard_map/all_to_all | solution.py:319
where the time goes:
time: 152 us; the launch traced here: 150 us
  blocking collectives  41.1 us (27%)
  starting transfers between devices  34.3 us (23%)
  waiting for transfers between devices  33.5 us (22%)
  Pallas kernels  25.9 us (17%)
  local copies, waits for them, and re-layouts  11.5 us (8%)
  other arithmetic  3.07 us (2%)
    all_to_all x1, blocking collectives, per_device(): lax.all_to_all(send, ('band', 'grid'), 0, 0, axis_index_groups=whole_plan...  24.6 us
    pallas_call x4, Pallas kernels, per_device(): call(functools.partial(step_kernel, mode), 'step', (field, message, messa...  14 us
    all_to_all x1, blocking collectives, per_device(): lax.all_to_all(copies, 'grid', 0, 0, axis_index_groups=members, tiled=True)  10.8 us
    ppermute x5, starting transfers between devices, exchange(): lax.ppermute(up, 'grid', [(i, (i + group) % grid) for i in range(grid)])  10.5 us
    all_to_all x1, waiting for transfers between devices, per_device(): lax.all_to_all(current, 'grid', 0, 0, axis_index_groups=in_plane, tiled=T...  10 us
    ppermute x5, waiting for transfers between devices, exchange(): lax.ppermute(up, 'grid', [(i, (i + group) % grid) for i in range(grid)])  9.73 us
    unnamed x11, local copies, waits for them, and re-layouts  9.44 us
    ppermute x5, starting transfers between devices, exchange(): lax.ppermute(down, 'grid', [(i, (i - group) % grid) for i in range(grid)])  9.24 us
  transfers between devices with their start and end apart: 13, of which 11 were waited for; matrix products, arithmetic and copies ran while one was open for 1% of the time, Pallas kernels for 4%

commit v1 on v0

v1 whole, which is shorter than its diff:
```python
import functools

import jax
import jax.numpy as jnp
from jax import lax
from jax.experimental import pallas as pl
from jax.experimental.pallas import tpu as pltpu
from jax.sharding import PartitionSpec as P

RADIUS = 4
DEGREE = 4
WINDOW = 17

stencil_weights = (-205.0 / 72.0, 1.6, -0.2, 8.0 / 315.0, -1.0 / 560.0)
filter_centre = 10.0
filter_half = 6.0

VMEM = pl.BlockSpec(memory_space=pltpu.VMEM)
SMEM = pl.BlockSpec(memory_space=pltpu.SMEM)
HBM = pl.BlockSpec(memory_space=pltpu.HBM)
NT = (((1,), (1,)), ((), ()))


def call(kernel, name, out_shape, in_specs, out_specs, scratch=(), flops=4_000_000, nbytes=2_000_000, vmem=6):
    return pl.pallas_call(
        kernel,
        name=name,
        out_shape=out_shape,
        in_specs=in_specs,
        out_specs=out_specs,
        scratch_shapes=list(scratch),
        compiler_params=pltpu.CompilerParams(vmem_limit_bytes=vmem << 20),
        cost_estimate=pl.CostEstimate(flops=flops, bytes_accessed=nbytes, transcendentals=0),
    )


def far(x):
    return pltpu.with_memory_space_constraint(x, pltpu.HBM)


def parcel_kernel(states, potential, out, held, extra, sems):
    group = out.shape[0]
    local = pltpu.make_async_copy(potential, extra, sems.at[2, 0])
    loads = [pltpu.make_async_copy(states.at[j], held.at[j], sems.at[0, j]) for j in range(group)]
    stores = [pltpu.make_async_copy(held.at[j], out.at[j, 0:2], sems.at[1, j]) for j in range(group)]
    extras = [pltpu.make_async_copy(extra, out.at[j, 2], sems.at[3, j]) for j in range(group)]
    for c in [local] + loads:
        c.start()
    local.wait()
    for c in extras:
        c.start()
    for j in range(group):
        loads[j].wait()
        stores[j].start()
    for c in extras + stores:
        c.wait()


def build_kernel(planes, info, idx_far, val_far, blocks_far, table, idx, val, blocks, sems):
    loads = [pltpu.make_async_copy(idx_far, idx, sems.at[0]), pltpu.make_async_copy(val_far, val, sems.at[1])]
    for c in loads:
        c.start()
    base = info[1, 1] * planes
    atoms, points = idx.shape
    cells = 8 * 128

    def pick(a, n):
        entry = info[0, a]
        table[0, n] = entry
        return n + (entry >= 0).astype(jnp.int32)

    count = lax.fori_loop(0, atoms, pick, jnp.int32(0), unroll=16)
    table[0, count] = atoms * 256
    pairs = (count + 1) >> 1
    table[1, 0] = pairs
    table[1, 1] = info[1, 1]
    table[1, 2] = info[1, 2]
    for c in loads:
        c.wait()
    sub = lax.broadcasted_iota(jnp.int32, (WINDOW * 8, points), 0)
    lane = lax.broadcasted_iota(jnp.int32, (128, points), 0)

    def pair(m, carry):
        for n in (2 * m, 2 * m + 1):
            entry = table[0, n]
            a = jnp.minimum(entry >> 8, atoms - 1)
            rel = idx[pl.ds(a, 1), :] - (base + (entry & 255)) * cells
            inside = (rel >= 0) & (rel < WINDOW * cells) & (n < count)
            w = jnp.where(inside, val[pl.ds(a, 1), :], 0.0)
            hit = sub == (rel >> 7)
            cols = (lane == (rel & 127)).astype(jnp.float32).astype(jnp.bfloat16)
            w1 = w.astype(jnp.bfloat16).astype(jnp.float32)
            w2 = (w - w1).astype(jnp.bfloat16).astype(jnp.float32)
            w3 = w - w1 - w2
            total = None
            for part in (w3, w2, w1):
                rows = jnp.where(hit, part, 0.0).astype(jnp.bfloat16)
                term = lax.dot_general(rows, cols, NT, preferred_element_type=jnp.float32)
                total = term if total is None else total + term
            blocks[pl.ds(n, 1)] = total.reshape(1, WINDOW, 8, 128)
        store(m).start()
        return carry

    def store(m):
        two = pl.ds(2 * m, 2)
        return pltpu.make_async_copy(blocks.at[two], blocks_far.at[two], sems.at[2 + m])

    def stored(m, carry):
        store(m).wait()
        return carry

    lax.fori_loop(0, pairs, pair, 0)
    lax.fori_loop(0, pairs, stored, 0)


def coefficients(table, field, blocks, sums, ready=None):
    atoms = blocks.shape[0]
    sums[...] = jnp.zeros_like(sums)

    def pair(m, carry):
        if ready is not None:
            ready(m)
        for n in (2 * m, 2 * m + 1):
            entry = table[0, n]
            b = blocks[n]
            for s in range(2):
                v = field[s, pl.ds(entry & 255, WINDOW)]
                sums[s, pl.ds(entry >> 8, 1), :] = jnp.sum(jnp.sum(b * v, axis=0), axis=0, keepdims=True)
        return carry

    lax.fori_loop(0, table[1, 0], pair, 0)
    ones = jnp.ones((8, 128), jnp.float32)
    return [
        lax.dot_general(
            ones, sums[s, 0:atoms], NT, precision=lax.Precision.HIGHEST, preferred_element_type=jnp.float32
        )
        for s in range(2)
    ]


def fill_messages(y, parts, up, down):
    planes = y.shape[1]
    for s in range(2):
        up[s, 0:4] = y[s, planes - 4 : planes]
        down[s, 0:4] = y[s, 0:4]
        up[s, 4] = parts[s]
        down[s, 4] = parts[s]


def first_kernel(table, got, blocks_far, y, up, down, blocks, sums, sems):
    def load(m):
        two = pl.ds(2 * m, 2)
        return pltpu.make_async_copy(blocks_far.at[two], blocks.at[two], sems.at[m])

    def begin(m, carry):
        load(m).start()
        return carry

    lax.fori_loop(0, table[1, 0], begin, 0)
    for s in range(2):
        for j in range(got.shape[0]):
            y[s, 8 * j : 8 * j + 8] = got[j, s]
    fill_messages(y, coefficients(table, y, blocks, sums, lambda m: load(m).wait()), up, down)


def lane_weights():
    lane = lax.broadcasted_iota(jnp.int32, (8, 128), 1)
    out = []
    for k in range(1, RADIUS + 1):
        c = stencil_weights[k]
        out.append((k, jnp.where(lane >= k, c, 0.0)))
        out.append((128 - k, jnp.where(lane < 128 - k, c, 0.0)))
    return out


def row_weights():
    row = lax.broadcasted_iota(jnp.int32, (8, 128), 0)
    out = []
    for r in range(1, 8):
        near = stencil_weights[r] if r <= RADIUS else 0.0
        far = stencil_weights[8 - r] if 8 - r <= RADIUS else 0.0
        out.append((r, jnp.where(row >= r, near, far)))
    return out


def scales(mode):
    if mode == "image":
        return 1.0, 0.0
    return (1.0 if mode == "first" else 2.0) / filter_half, filter_centre


def stencil_kernel(mode, y, *refs):
    has_prev = mode == "later"
    prev, v, out, pad = refs if has_prev else (None, *refs)
    alpha, sigma = scales(mode)
    planes = y.shape[1]
    for s in range(2):
        pad[s, 0:4] = jnp.zeros((4, 8, 128), jnp.float32)
        pad[s, 4 : planes + 4] = y[s]
        pad[s, planes + 4 : planes + 8] = jnp.zeros((4, 8, 128), jnp.float32)
    half = -0.5 * alpha
    lanes = [(k, w * half) for k, w in lane_weights()]
    rows = [(k, w * half) for k, w in row_weights()]
    centre = half * 3.0 * stencil_weights[0] - alpha * sigma

    def block(j, carry):
        for s in range(2):
            line = [pad[s, 8 * j + t] for t in range(16)]
            for t in range(8):
                mid = line[t + 4]
                acc = (alpha * v[j, 2, t] + centre) * mid
                for k in range(1, RADIUS + 1):
                    acc = acc + (half * stencil_weights[k]) * (line[t + 4 + k] + line[t + 4 - k])
                for k, w in rows:
                    acc = acc + w * pltpu.roll(mid, k, 0)
                for k, w in lanes:
                    acc = acc + w * pltpu.roll(mid, k, 1)
                if has_prev:
                    acc = acc - prev[s, 8 * j + t]
                out[s, 8 * j + t] = acc
        return carry

    lax.fori_loop(0, planes // 8, block, 0)


def finish_kernel(mode, table, partial, blocks, strength, below, above, own, *refs):
    alpha, sigma = scales(mode)
    if mode == "image":
        y, send, new, splat = refs
    else:
        new, up, down, splat, sums = refs
    planes = partial.shape[1]
    atoms = blocks.shape[0]
    z = table[1, 1]
    has_low = z > 0
    has_high = z < lax.axis_size("grid") // (planes // 8) - 1
    half = -0.5 * alpha

    for s in range(2):
        total = (own[s, 4] + below[s, 4] + above[s, 4]) * strength[...] * alpha
        splat[s, 0:atoms] = jnp.transpose(jnp.broadcast_to(total[0:1], (128, 128)))
        splat[s, atoms : atoms + 8] = jnp.zeros((8, 128), jnp.float32)

    new[...] = partial[...]
    for s in range(2):
        low = [jnp.where(has_low, below[s, i], 0.0) for i in range(4)]
        high = [jnp.where(has_high, above[s, i], 0.0) for i in range(4)]
        for t in range(4):
            for side, edge in ((low, 0), (high, 1)):
                acc = None
                for k in range(t + 1, RADIUS + 1):
                    value = side[t - k + 4] if edge == 0 else side[k - t - 1]
                    term = (half * stencil_weights[k]) * value
                    acc = term if acc is None else acc + term
                p = t if edge == 0 else planes - 1 - t
                new[s, p] = new[s, p] + acc

    def spread(m, carry):
        for n in (2 * m, 2 * m + 1):
            entry = table[0, n]
            b = blocks[n]
            window = pl.ds(entry & 255, WINDOW)
            for s in range(2):
                c = jnp.broadcast_to(splat[s, pl.ds(entry >> 8, 1), :], (8, 128))
                new[s, window] = new[s, window] + c * b
        return carry

    lax.fori_loop(0, table[1, 0], spread, 0)

    if mode == "image":
        for s in range(2):
            for p in range(planes):
                j, t = divmod(p, 8)
                d = (t // 2) * (planes // 8) + j
                q = 8 * (t % 2)
                send[d, s, 0, q : q + 8] = y[s, p]
                send[d, s, 1, q : q + 8] = new[s, p]
    else:
        fill_messages(new, coefficients(table, new, blocks, sums), up, down)


def product_kernel(table, got, keep, give, rows):
    states = rows.shape[0]
    total = None
    for r in range(0, 16, 2):
        f = [got[pl.ds(r + i, states, stride=32), :] for i in range(2)]
        h = [got[pl.ds(16 + r + i, states, stride=32), :] for i in range(2)]
        f = jnp.concatenate(f, axis=1)
        left = jnp.concatenate([f, jnp.concatenate(h, axis=1)], axis=0)
        term = lax.dot_general(
            left, f, NT, precision=lax.Precision.HIGHEST, preferred_element_type=jnp.float32
        )
        total = term if total is None else total + term
    rows[...] = jnp.concatenate([total[0:states], total[states : 2 * states]], axis=1)
    band = table[1, 2]
    size = keep.shape[1]
    for other in range(2):
        chip = band ^ (2 * other)
        keep[other] = rows[pl.ds(pl.multiple_of(chip * size, size), size), :]
        give[other] = rows[pl.ds(pl.multiple_of((chip ^ 1) * size, size), size), :]


def pack_kernel(y, parts, out):
    rows = parts[0]
    for k in range(1, parts.shape[0]):
        rows = rows + parts[k]
    for j in range(out.shape[0]):
        out[j, 0:8] = y[0, 8 * j : 8 * j + 8]
        out[j, 8:16] = y[1, 8 * j : 8 * j + 8]
        out[j, 16] = rows[0:8]
        out[j, 17] = rows[8:16]


def unpack_kernel(scale, got, filtered, gram, hamiltonian):
    width = gram.shape[1]
    for half in range(2):
        rows = got[0, 16 + half]
        for j in range(1, got.shape[0]):
            rows = rows + got[j, 16 + half]
        rows = rows * scale
        gram[8 * half : 8 * half + 8] = rows[:, 0:width]
        hamiltonian[8 * half : 8 * half + 8] = rows[:, width : 2 * width]
    for j in range(got.shape[0]):
        filtered[2 * j] = got[j, 0:8]
        filtered[2 * j + 1] = got[j, 8:16]


def per_device(states, potential, proj_index, proj_value, proj_strength):
    f32 = jnp.float32
    shape = jax.ShapeDtypeStruct
    count, depth, ny, nz = states.shape
    atoms = proj_index.shape[0]
    grid = lax.axis_size("grid")
    bands = lax.axis_size("band")
    group = 8
    zs = grid // group
    per = count // group
    planes = group * depth
    everyone = bands * count
    in_plane = [[z * group + j for j in range(group)] for z in range(zs)]
    along_z = [[z * group + j for z in range(zs)] for j in range(group)]
    whole_plane = [[b * grid + z * group + j for b in range(bands) for j in range(group)] for z in range(zs)]

    parcel = call(
        parcel_kernel,
        "parcel",
        pltpu.HBM((group, 3, depth, ny, nz), f32),
        [HBM] * 2,
        HBM,
        [
            pltpu.VMEM((group, per, depth, ny, nz), f32),
            pltpu.VMEM((depth, ny, nz), f32),
            pltpu.SemaphoreType.DMA((4, group)),
        ],
    )(far(states.reshape(group, per, depth, ny, nz)), far(potential))
    start = lax.all_to_all(parcel, "grid", 0, 0, axis_index_groups=in_plane, tiled=True)

    place = lax.axis_index("grid") // group
    support = proj_index >> 10
    low = jnp.min(support, axis=1) - place * planes
    high = jnp.max(support, axis=1) - place * planes
    entry = jnp.arange(atoms, dtype=jnp.int32) * 256 + jnp.clip(low, 0, planes - WINDOW)
    entry = jnp.where((high >= 0) & (low < planes), entry, -1)
    lane = jnp.arange(atoms, dtype=jnp.int32)
    where = jnp.where(lane == 1, place, jnp.where(lane == 2, lax.axis_index("band"), 0))
    info = jnp.stack([entry, where]).astype(jnp.int32)

    field = shape((per, planes, ny, nz), f32)
    message = shape((per, 5, ny, nz), f32)
    sums = pltpu.VMEM((per, atoms + 8, 128), f32)
    pad = pltpu.VMEM((per, planes + 8, ny, nz), f32)
    new = pltpu.VMEM(field.shape, f32)
    strength = proj_strength.reshape(1, atoms)

    block = (atoms, WINDOW, ny, nz)
    blocks_far, table = call(
        functools.partial(build_kernel, planes),
        "build",
        (pltpu.HBM(block, f32), shape((2, 256), jnp.int32)),
        [SMEM, HBM, HBM],
        (HBM, SMEM),
        [
            pltpu.VMEM(proj_index.shape, jnp.int32),
            pltpu.VMEM(proj_value.shape, f32),
            pltpu.VMEM(block, f32),
            pltpu.SemaphoreType.DMA((2 + atoms // 2,)),
        ],
        vmem=16,
    )(info, far(proj_index), far(proj_value))
    current, up, down, blocks = call(
        first_kernel,
        "first",
        (field, message, message, shape(block, f32)),
        [SMEM, VMEM, HBM],
        (VMEM,) * 4,
        [sums, pltpu.SemaphoreType.DMA((atoms // 2,))],
        vmem=16,
    )(table, start, far(blocks_far))

    def exchange(up, down):
        below = lax.ppermute(up, "grid", [(i, (i + group) % grid) for i in range(grid)])
        above = lax.ppermute(down, "grid", [(i, (i - group) % grid) for i in range(grid)])
        return below, above

    def local(mode, *arrays):
        return call(
            functools.partial(stencil_kernel, mode), "stencil", field, [VMEM] * len(arrays), VMEM, [pad]
        )(*arrays)

    previous = None
    for k in range(DEGREE):
        mode = "later" if k else "first"
        below, above = exchange(up, down)
        partial = local(mode, current, *([previous] if k else []), start)
        following, up, down = call(
            functools.partial(finish_kernel, mode),
            "finish",
            (field, message, message),
            [SMEM] + [VMEM] * 6,
            (VMEM,) * 3,
            [sums, sums],
        )(table, partial, blocks, strength, below, above, up)
        previous, current = current, following

    below, above = exchange(up, down)
    send = call(
        functools.partial(finish_kernel, "image"),
        "image",
        shape((bands * group, per, 2, 2 * ny, nz), f32),
        [SMEM] + [VMEM] * 7,
        VMEM,
        [new, sums],
    )(table, local("image", current, start), blocks, strength, below, above, up, current)
    got = lax.all_to_all(send, ("band", "grid"), 0, 0, axis_index_groups=whole_plane, tiled=True)
    half = shape((2, count, 2 * everyone), f32)
    keep, give = call(
        product_kernel, "product", (half, half), [SMEM, VMEM], (VMEM, VMEM), [pltpu.VMEM((everyone, 2 * everyone), f32)]
    )(table, got.reshape(everyone * 32, nz))
    keep = keep + lax.ppermute(give, "band", [(i, i ^ 1) for i in range(bands)])
    rows = keep[0] + lax.ppermute(keep[1], "band", [(i, i ^ 2) for i in range(bands)])

    copies = jnp.broadcast_to(rows, (zs, *rows.shape))
    copies = lax.all_to_all(copies, "grid", 0, 0, axis_index_groups=along_z, tiled=True)
    packed = call(pack_kernel, "pack", shape((group, 18, ny, nz), f32), [VMEM, VMEM], VMEM)(current, copies)
    packed = lax.all_to_all(packed, "grid", 0, 0, axis_index_groups=in_plane, tiled=True)
    square = shape((count, everyone), f32)
    return call(
        functools.partial(unpack_kernel, 1.0 / float(grid * depth * ny * nz)),
        "unpack",
        (shape(states.shape, f32), square, square),
        [VMEM],
        (VMEM,) * 3,
    )(packed)


def solution(mesh):
    in_specs = (P("band", "grid", None, None), P("grid", None, None), P(), P(), P())
    out_specs = (P("band", "grid", None, None), P("band", None), P("band", None))
    return jax.shard_map(
        per_device, mesh=mesh, in_specs=in_specs, out_specs=out_specs, check_vma=False
    )
```

time: 152 us -> 123 us (0.81)
  waiting for transfers between devices: 33.5 us -> 20 us
  starting transfers between devices: 34.3 us -> 21.7 us
  local copies, waits for them, and re-layouts: 11.5 us -> 0.02 us
  blocking collectives: 41.1 us -> 48.7 us
  Pallas kernels: 25.9 us -> 29.9 us
  other arithmetic: 3.07 us -> 0.97 us
    all_to_all x2 -> x0, waiting for transfers between devices: 18.4 us -> none  [the longest x1 10 us: per_device(): lax.all_to_all(current, 'grid', 0, 0, axis_index_groups=in_plane, tiled=T...]
    all_to_all x2, blocking collectives: 16.5 us -> 28 us  [the longest x1 14.3 us: per_device(): lax.all_to_all(packed, 'grid', 0, 0, axis_index_groups=in_plane, tiled=True)]
    unnamed x11 -> x2, local copies, waits for them, and re-layouts: 9.44 us -> 0.01 us
    all_to_all x2 -> x0, starting transfers between devices: 8.5 us -> none  [the longest x1 5.01 us: per_device(): lax.all_to_all(copies, 'grid', 0, 0, axis_index_groups=members, tiled=True)]
    all_to_all x1, waiting for transfers between devices: 1.23 us -> 6.53 us  [per_device(): lax.all_to_all(parcel, 'grid', 0, 0, axis_index_groups=in_plane, tiled=True)]
    pallas_call x8 -> x16, Pallas kernels: 25.9 us -> 29.9 us  [the longest x5 8.46 us: local(): call(functools.partial(stencil_kernel, mode), 'stencil', field, [VMEM] *...]
    all_to_all x1, blocking collectives: 24.6 us -> 20.8 us  [per_device(): lax.all_to_all(send, ('band', 'grid'), 0, 0, axis_index_groups=whole_plan...]
    ppermute x0 -> x2, waiting for transfers between devices: none -> 3.39 us  [the longest x1 2.22 us: per_device(): lax.ppermute(keep[1], 'band', [(i, i ^ 2) for i in range(bands)])]
  transfers between devices with their start and end apart: 13 -> 13, of which waited for: 11 -> 12; matrix products, arithmetic and copies ran while one was open for 1% -> 1% of each run, Pallas kernels for 4% -> 12%
where the time goes in v1:
time: 123 us; the launch traced here: 122 us
  blocking collectives  48.7 us (40%)
  Pallas kernels  29.9 us (24%)
  starting transfers between devices  21.7 us (18%)
  waiting for transfers between devices  20 us (16%)
    all_to_all x1, blocking collectives, per_device(): lax.all_to_all(send, ('band', 'grid'), 0, 0, axis_index_groups=whole_plan...  20.8 us
    all_to_all x1, blocking collectives, per_device(): lax.all_to_all(packed, 'grid', 0, 0, axis_index_groups=in_plane, tiled=True)  14.3 us
    all_to_all x1, blocking collectives, per_device(): lax.all_to_all(copies, 'grid', 0, 0, axis_index_groups=along_z, tiled=True)  13.6 us
    ppermute x5, waiting for transfers between devices, exchange(): lax.ppermute(up, 'grid', [(i, (i + group) % grid) for i in range(grid)])  8.82 us
    pallas_call x5, Pallas kernels, local(): call(functools.partial(stencil_kernel, mode), 'stencil', field, [VMEM] *...  8.46 us
    ppermute x5, starting transfers between devices, exchange(): lax.ppermute(up, 'grid', [(i, (i + group) % grid) for i in range(grid)])  7.89 us
    pallas_call x4, Pallas kernels, per_device(): call(functools.partial(finish_kernel, mode), 'finish', (field, message, m...  6.63 us
    all_to_all x1, waiting for transfers between devices, per_device(): lax.all_to_all(parcel, 'grid', 0, 0, axis_index_groups=in_plane, tiled=True)  6.53 us
  transfers between devices with their start and end apart: 13, of which 12 were waited for; matrix products, arithmetic and copies ran while one was open for 1% of the time, Pallas kernels for 12%

profile of v1, /device:TPU:2, one launch (start us, length us, event | category | flops | bytes accessed | tf_op | source)
XLA Modules:
  0.0 122.1 jit_solution(15622451642684449890)
XLA Ops:
  0.6 2.0 %parcel.1 = f32[8,3,8,8,128]{4,3,2,1,0:T(8,128)} custom-call(f32[8,2,8,8,128]{4,3,2,1,0:T(8,128)} %bitcast.21, f32[8,8,128]{2,1,0:T(8,128)} %potential.1), custom_call_target="tpu_custom_call" | custom-call | flops 4000000 | bytes 2000000 | tf_op jit(solution)/shard_map/parcel/pallas_call | solution.py:344
  2.7 6.0 %all-to-all-start = ((f32[8,3,8,8,128]{4,3,2,1,0:T(8,128)}), f32[8,3,8,8,128]{4,3,2,1,0:T(8,128)S(1)}, u32[]{:S(2)}, u32[]{:S(2)}) async-start(f32[8,3,8,8,128]{4,3,2,1,0:T(8,128)} %parcel.1), calls=%async_computation | async-start | bytes 1572864 | tf_op jit(solution)/shard_map/all_to_all | solution.py:356
  9.7 5.9 %build.1 = (f32[128,17,8,128]{3,2,1,0:T(8,128)}, s32[2,256]{1,0:T(2,128)S(1)}) custom-call(s32[2,128]{1,0:T(2,128)S(1)} %pad_add_fusion.info, s32[128,128]{1,0:T(8,128)} %idx_far.1, f32[128,128]{1,0:T(8,128)} %val_far.1), custom_call_target="tpu_custom_call" | custom-call | flops 4000000 | bytes 2000000 | tf_op jit(solution)/shard_map/build/pallas_call | solution.py:376
  15.6 6.5 %all-to-all-done.got.refs_0_.refs_1_ = f32[8,3,8,8,128]{4,3,2,1,0:T(8,128)S(1)} async-done(((f32[8,3,8,8,128]{4,3,2,1,0:T(8,128)}), f32[8,3,8,8,128]{4,3,2,1,0:T(8,128)S(1)}, u32[]{:S(2)}, u32[]{:S(2)}) %all-to-all-start) | async-done | bytes 786464 | tf_op jit(solution)/shard_map/all_to_all | solution.py:356
  22.1 2.9 %first.1 = (f32[2,64,8,128]{3,2,1,0:T(8,128)S(1)}, f32[2,5,8,128]{3,2,1,0:T(8,128)S(1)}, f32[2,5,8,128]{3,2,1,0:T(8,128)S(1)}, f32[128,17,8,128]{3,2,1,0:T(8,128)S(1)}) custom-call(s32[2,256]{1,0:T(2,128)S(1)} %get-tuple-element.23.table, f32[8,3,8,8,128]{4,3,2,1,0:T(8,128)S(1)} %all-to-all-done.got.refs_0_.refs_1_, ...), custom_call_target="tpu_custom_call" | custom-call | flops 4000000 | bytes 2000000 | tf_op jit(solution)/shard_map/first/pallas_call | solution.py:390
  25.0 6.0 %collective-permute-start.1 = (f32[2,5,8,128]{3,2,1,0:T(8,128)S(1)}, f32[2,5,8,128]{3,2,1,0:T(8,128)S(1)}, u32[]{:S(2)}, u32[]{:S(2)}) collective-permute-start(f32[2,5,8,128]{3,2,1,0:T(8,128)S(1)} %get-tuple-element.28), channel_id=1, source_target_pairs={{0,56},{1,57},{2,58},{3,59},{4,60},{5,61},{6,62},{7,63},{8,0},{9,1... | collective-permute-start | bytes 122888 | tf_op jit(solution)/shard_map/ppermute | solution.py:402
  30.9 1.7 %stencil.5.partial = f32[2,64,8,128]{3,2,1,0:T(8,128)S(1)} custom-call(f32[2,64,8,128]{3,2,1,0:T(8,128)S(1)} %get-tuple-element.25.y.refs_0_, f32[8,3,8,8,128]{4,3,2,1,0:T(8,128)S(1)} %all-to-all-done.got.refs_0_.refs_1_), custom_call_target="tpu_custom_call" | custom-call | flops 4000000 | bytes 2000000 | tf_op jit(solution)/shard_map/stencil/pallas_call | solution.py:406
  32.7 3.5 %collective-permute-done.below = f32[2,5,8,128]{3,2,1,0:T(8,128)S(1)} collective-permute-done((f32[2,5,8,128]{3,2,1,0:T(8,128)S(1)}, f32[2,5,8,128]{3,2,1,0:T(8,128)S(1)}, u32[]{:S(2)}, u32[]{:S(2)}) %collective-permute-start) | collective-permute-done | bytes 40992 | tf_op jit(solution)/shard_map/ppermute | solution.py:401
  36.2 1.7 %finish.4 = (f32[2,64,8,128]{3,2,1,0:T(8,128)S(1)}, f32[2,5,8,128]{3,2,1,0:T(8,128)S(1)}, f32[2,5,8,128]{3,2,1,0:T(8,128)S(1)}) custom-call(s32[2,256]{1,0:T(2,128)S(1)} %get-tuple-element.23.table, f32[2,64,8,128]{3,2,1,0:T(8,128)S(1)} %stencil.5.partial, f32[128,17,8,128]{3,2,1,0:T(8,128)S(1)} %get-tuple-element.26.blocks, f32[1,128]{1,0:T(1,128)S(1)} %bitcast.16, ...), custom_call_target="tpu_custom_call" | custom-call | flops 4000000 | bytes 2000000 | tf_op jit(solution)/shard_map/finish/pallas_call | solution.py:415
  37.9 2.0 %collective-permute-start.2 = (f32[2,5,8,128]{3,2,1,0:T(8,128)S(1)}, f32[2,5,8,128]{3,2,1,0:T(8,128)S(1)}, u32[]{:S(2)}, u32[]{:S(2)}) collective-permute-start(f32[2,5,8,128]{3,2,1,0:T(8,128)S(1)} %get-tuple-element.30.own), channel_id=1, source_target_pairs={{0,8},{1,9},{2,10},{3,11},{4,12},{5,13},{6,14},{7,15},{8,16},{9,17... | collective-permute-start | bytes 122888 | tf_op jit(solution)/shard_map/ppermute | solution.py:401
  39.9 1.7 %stencil.6.partial = f32[2,64,8,128]{3,2,1,0:T(8,128)S(1)} custom-call(f32[2,64,8,128]{3,2,1,0:T(8,128)S(1)} %get-tuple-element.29.y.refs_0_, f32[2,64,8,128]{3,2,1,0:T(8,128)S(1)} %get-tuple-element.25.y.refs_0_, f32[8,3,8,8,128]{4,3,2,1,0:T(8,128)S(1)} %all-to-all-done.got.refs_0_.refs_1_), custom_call_target="tpu_custom_call" | custom-call | flops 4000000 | bytes 2000000 | tf_op jit(solution)/shard_map/stencil/pallas_call | solution.py:406
  41.8 1.3 %collective-permute-done.2.below = f32[2,5,8,128]{3,2,1,0:T(8,128)S(1)} collective-permute-done((f32[2,5,8,128]{3,2,1,0:T(8,128)S(1)}, f32[2,5,8,128]{3,2,1,0:T(8,128)S(1)}, u32[]{:S(2)}, u32[]{:S(2)}) %collective-permute-start.2) | collective-permute-done | bytes 40992 | tf_op jit(solution)/shard_map/ppermute | solution.py:401
  43.1 1.7 %finish.5 = (f32[2,64,8,128]{3,2,1,0:T(8,128)S(1)}, f32[2,5,8,128]{3,2,1,0:T(8,128)S(1)}, f32[2,5,8,128]{3,2,1,0:T(8,128)S(1)}) custom-call(s32[2,256]{1,0:T(2,128)S(1)} %get-tuple-element.23.table, f32[2,64,8,128]{3,2,1,0:T(8,128)S(1)} %stencil.6.partial, f32[128,17,8,128]{3,2,1,0:T(8,128)S(1)} %get-tuple-element.26.blocks, f32[1,128]{1,0:T(1,128)S(1)} %bitcast.17, ...), custom_call_target="tpu_custom_call" | custom-call | flops 4000000 | bytes 2000000 | tf_op jit(solution)/shard_map/finish/pallas_call | solution.py:415
  44.9 2.0 %collective-permute-start.4 = (f32[2,5,8,128]{3,2,1,0:T(8,128)S(1)}, f32[2,5,8,128]{3,2,1,0:T(8,128)S(1)}, u32[]{:S(2)}, u32[]{:S(2)}) collective-permute-start(f32[2,5,8,128]{3,2,1,0:T(8,128)S(1)} %get-tuple-element.33.own), channel_id=1, source_target_pairs={{0,8},{1,9},{2,10},{3,11},{4,12},{5,13},{6,14},{7,15},{8,16},{9,17... | collective-permute-start | bytes 122888 | tf_op jit(solution)/shard_map/ppermute | solution.py:401
  46.8 1.7 %stencil.7.partial = f32[2,64,8,128]{3,2,1,0:T(8,128)S(1)} custom-call(f32[2,64,8,128]{3,2,1,0:T(8,128)S(1)} %get-tuple-element.32.y.refs_0_, f32[2,64,8,128]{3,2,1,0:T(8,128)S(1)} %get-tuple-element.29.y.refs_0_, f32[8,3,8,8,128]{4,3,2,1,0:T(8,128)S(1)} %all-to-all-done.got.refs_0_.refs_1_), custom_call_target="tpu_custom_call" | custom-call | flops 4000000 | bytes 2000000 | tf_op jit(solution)/shard_map/stencil/pallas_call | solution.py:406
  48.8 1.3 %collective-permute-done.4.below = f32[2,5,8,128]{3,2,1,0:T(8,128)S(1)} collective-permute-done((f32[2,5,8,128]{3,2,1,0:T(8,128)S(1)}, f32[2,5,8,128]{3,2,1,0:T(8,128)S(1)}, u32[]{:S(2)}, u32[]{:S(2)}) %collective-permute-start.4) | collective-permute-done | bytes 40992 | tf_op jit(solution)/shard_map/ppermute | solution.py:401
  50.1 1.6 %finish.6 = (f32[2,64,8,128]{3,2,1,0:T(8,128)S(1)}, f32[2,5,8,128]{3,2,1,0:T(8,128)S(1)}, f32[2,5,8,128]{3,2,1,0:T(8,128)S(1)}) custom-call(s32[2,256]{1,0:T(2,128)S(1)} %get-tuple-element.23.table, f32[2,64,8,128]{3,2,1,0:T(8,128)S(1)} %stencil.7.partial, f32[128,17,8,128]{3,2,1,0:T(8,128)S(1)} %get-tuple-element.26.blocks, f32[1,128]{1,0:T(1,128)S(1)} %bitcast.18, ...), custom_call_target="tpu_custom_call" | custom-call | flops 4000000 | bytes 2000000 | tf_op jit(solution)/shard_map/finish/pallas_call | solution.py:415
  51.9 1.9 %collective-permute-start.6 = (f32[2,5,8,128]{3,2,1,0:T(8,128)S(1)}, f32[2,5,8,128]{3,2,1,0:T(8,128)S(1)}, u32[]{:S(2)}, u32[]{:S(2)}) collective-permute-start(f32[2,5,8,128]{3,2,1,0:T(8,128)S(1)} %get-tuple-element.36.own), channel_id=1, source_target_pairs={{0,8},{1,9},{2,10},{3,11},{4,12},{5,13},{6,14},{7,15},{8,16},{9,17... | collective-permute-start | bytes 122888 | tf_op jit(solution)/shard_map/ppermute | solution.py:401
  53.8 1.7 %stencil.8.partial = f32[2,64,8,128]{3,2,1,0:T(8,128)S(1)} custom-call(f32[2,64,8,128]{3,2,1,0:T(8,128)S(1)} %get-tuple-element.35.y, f32[2,64,8,128]{3,2,1,0:T(8,128)S(1)} %get-tuple-element.32.y.refs_0_, f32[8,3,8,8,128]{4,3,2,1,0:T(8,128)S(1)} %all-to-all-done.got.refs_0_.refs_1_), custom_call_target="tpu_custom_call" | custom-call | flops 4000000 | bytes 2000000 | tf_op jit(solution)/shard_map/stencil/pallas_call | solution.py:406
  55.9 1.5 %collective-permute-done.6.below = f32[2,5,8,128]{3,2,1,0:T(8,128)S(1)} collective-permute-done((f32[2,5,8,128]{3,2,1,0:T(8,128)S(1)}, f32[2,5,8,128]{3,2,1,0:T(8,128)S(1)}, u32[]{:S(2)}, u32[]{:S(2)}) %collective-permute-start.6) | collective-permute-done | bytes 40992 | tf_op jit(solution)/shard_map/ppermute | solution.py:401
  57.4 1.7 %finish.7 = (f32[2,64,8,128]{3,2,1,0:T(8,128)S(1)}, f32[2,5,8,128]{3,2,1,0:T(8,128)S(1)}, f32[2,5,8,128]{3,2,1,0:T(8,128)S(1)}) custom-call(s32[2,256]{1,0:T(2,128)S(1)} %get-tuple-element.23.table, f32[2,64,8,128]{3,2,1,0:T(8,128)S(1)} %stencil.8.partial, f32[128,17,8,128]{3,2,1,0:T(8,128)S(1)} %get-tuple-element.26.blocks, f32[1,128]{1,0:T(1,128)S(1)} %bitcast.19, ...), custom_call_target="tpu_custom_call" | custom-call | flops 4000000 | bytes 2000000 | tf_op jit(solution)/shard_map/finish/pallas_call | solution.py:415
  59.1 2.0 %collective-permute-start.8 = (f32[2,5,8,128]{3,2,1,0:T(8,128)S(1)}, f32[2,5,8,128]{3,2,1,0:T(8,128)S(1)}, u32[]{:S(2)}, u32[]{:S(2)}) collective-permute-start(f32[2,5,8,128]{3,2,1,0:T(8,128)S(1)} %get-tuple-element.39.own), channel_id=1, source_target_pairs={{0,8},{1,9},{2,10},{3,11},{4,12},{5,13},{6,14},{7,15},{8,16},{9,17... | collective-permute-start | bytes 122888 | tf_op jit(solution)/shard_map/ppermute | solution.py:401
  61.1 1.7 %stencil.9.partial = f32[2,64,8,128]{3,2,1,0:T(8,128)S(1)} custom-call(f32[2,64,8,128]{3,2,1,0:T(8,128)S(1)} %get-tuple-element.38.y.refs_0_, f32[8,3,8,8,128]{4,3,2,1,0:T(8,128)S(1)} %all-to-all-done.got.refs_0_.refs_1_), custom_call_target="tpu_custom_call" | custom-call | flops 4000000 | bytes 2000000 | tf_op jit(solution)/shard_map/stencil/pallas_call | solution.py:406
  63.1 1.3 %collective-permute-done.8.below = f32[2,5,8,128]{3,2,1,0:T(8,128)S(1)} collective-permute-done((f32[2,5,8,128]{3,2,1,0:T(8,128)S(1)}, f32[2,5,8,128]{3,2,1,0:T(8,128)S(1)}, u32[]{:S(2)}, u32[]{:S(2)}) %collective-permute-start.8) | collective-permute-done | bytes 40992 | tf_op jit(solution)/shard_map/ppermute | solution.py:401
  64.4 1.0 image.1
  65.4 20.8 %all_to_all.20 = f32[32,2,2,16,128]{4,3,2,1,0:T(8,128)S(1)} all-to-all(f32[32,2,2,16,128]{4,3,2,1,0:T(8,128)S(1)} %image.1), channel_id=1, replica_groups={{0,1,2,3,4,5,6,7,64,65,66,67,68,69,70,71,128,129,130,131,132,133,134,13..., dimensions={0} | all-to-all | bytes 2097152 | tf_op jit(solution)/shard_map/all_to_all | solution.py:434
  86.2 2.1 %product.1 = (f32[2,16,128]{2,1,0:T(8,128)S(1)}, f32[2,16,128]{2,1,0:T(8,128)S(1)}) custom-call(s32[2,256]{1,0:T(2,128)S(1)} %get-tuple-element.23.table, f32[2048,128]{1,0:T(8,128)S(1)} %bitcast.15), custom_call_target="tpu_custom_call" | custom-call | flops 4000000 | bytes 2000000 | tf_op jit(solution)/shard_map/product/pallas_call | solution.py:436
  88.4 1.2 collective-permute-done.10
  89.6 1.4 %collective-permute-start.11 = (f32[16,128]{1,0:T(8,128)S(1)}, f32[16,128]{1,0:T(8,128)S(1)}, u32[]{:S(2)}, u32[]{:S(2)}) collective-permute-start(f32[16,128]{1,0:T(8,128)S(1)} %slice_bitcast_fusion), channel_id=1, source_target_pairs={{0,128},{64,192},{128,0},{192,64},{1,129},{65,193},{129,1},{193,65... | collective-permute-start | bytes 24584 | tf_op jit(solution)/shard_map/ppermute | solution.py:440
  91.0 2.2 %collective-permute-done.11 = f32[16,128]{1,0:T(8,128)S(1)} collective-permute-done((f32[16,128]{1,0:T(8,128)S(1)}, f32[16,128]{1,0:T(8,128)S(1)}, u32[]{:S(2)}, u32[]{:S(2)}) %collective-permute-start.11) | collective-permute-done | bytes 8224 | tf_op jit(solution)/shard_map/ppermute | solution.py:440
  93.2 13.6 %all_to_all.21.parts = f32[8,16,128]{2,1,0:T(8,128)S(1)} all-to-all(f32[8,16,128]{2,1,0:T(8,128)S(1)} %broadcast_in_dim.20), channel_id=1, replica_groups={{0,8,16,24,32,40,48,56},{1,9,17,25,33,41,49,57},{2,10,18,26,34,42,50,58..., dimensions={0} | all-to-all | bytes 131072 | tf_op jit(solution)/shard_map/all_to_all | solution.py:443
  106.9 14.3 %all_to_all.22.got = f32[8,18,8,128]{3,2,1,0:T(8,128)S(1)} all-to-all(f32[8,18,8,128]{3,2,1,0:T(8,128)S(1)} %pack.1), channel_id=1, replica_groups={{0,1,2,3,4,5,6,7},{8,9,10,11,12,13,14,15},{16,17,18,19,20,21,22,23},{24..., dimensions={0} | all-to-all | bytes 1179648 | tf_op jit(solution)/shard_map/all_to_all | solution.py:445
  (22 shorter events, 3.5 us)
Async XLA Ops:
  0.6 35.5 %copy-start = (f32[128]{0:T(128)S(1)}, f32[128]{0:T(128)}, u32[]{:S(2)}) copy-start(f32[128]{0:T(128)} %param.9) | copy-start | bytes 1540
  2.7 19.4 %all-to-all-start = ((f32[8,3,8,8,128]{4,3,2,1,0:T(8,128)}), f32[8,3,8,8,128]{4,3,2,1,0:T(8,128)S(1)}, u32[]{:S(2)}, u32[]{:S(2)}) async-start(f32[8,3,8,8,128]{4,3,2,1,0:T(8,128)} %parcel.1), calls=%async_computation | async-start | bytes 1572864 | tf_op jit(solution)/shard_map/all_to_all | solution.py:356
  25.0 7.7 %collective-permute-start.1 = (f32[2,5,8,128]{3,2,1,0:T(8,128)S(1)}, f32[2,5,8,128]{3,2,1,0:T(8,128)S(1)}, u32[]{:S(2)}, u32[]{:S(2)}) collective-permute-start(f32[2,5,8,128]{3,2,1,0:T(8,128)S(1)} %get-tuple-element.28), channel_id=1, source_target_pairs={{0,56},{1,57},{2,58},{3,59},{4,60},{5,61},{6,62},{7,63},{8,0},{9,1... | collective-permute-start | bytes 122888 | tf_op jit(solution)/shard_map/ppermute | solution.py:402
  30.9 5.2 %collective-permute-start = (f32[2,5,8,128]{3,2,1,0:T(8,128)S(1)}, f32[2,5,8,128]{3,2,1,0:T(8,128)S(1)}, u32[]{:S(2)}, u32[]{:S(2)}) collective-permute-start(f32[2,5,8,128]{3,2,1,0:T(8,128)S(1)} %get-tuple-element.27.own), channel_id=1, source_target_pairs={{0,8},{1,9},{2,10},{3,11},{4,12},{5,13},{6,14},{7,15},{8,16},{9,17... | collective-permute-start | bytes 122888 | tf_op jit(solution)/shard_map/ppermute | solution.py:401
  37.8 4.0 %collective-permute-start.3 = (f32[2,5,8,128]{3,2,1,0:T(8,128)S(1)}, f32[2,5,8,128]{3,2,1,0:T(8,128)S(1)}, u32[]{:S(2)}, u32[]{:S(2)}) collective-permute-start(f32[2,5,8,128]{3,2,1,0:T(8,128)S(1)} %get-tuple-element.31), channel_id=1, source_target_pairs={{0,56},{1,57},{2,58},{3,59},{4,60},{5,61},{6,62},{7,63},{8,0},{9,1... | collective-permute-start | bytes 122888 | tf_op jit(solution)/shard_map/ppermute | solution.py:402
  37.9 5.2 %collective-permute-start.2 = (f32[2,5,8,128]{3,2,1,0:T(8,128)S(1)}, f32[2,5,8,128]{3,2,1,0:T(8,128)S(1)}, u32[]{:S(2)}, u32[]{:S(2)}) collective-permute-start(f32[2,5,8,128]{3,2,1,0:T(8,128)S(1)} %get-tuple-element.30.own), channel_id=1, source_target_pairs={{0,8},{1,9},{2,10},{3,11},{4,12},{5,13},{6,14},{7,15},{8,16},{9,17... | collective-permute-start | bytes 122888 | tf_op jit(solution)/shard_map/ppermute | solution.py:401
  44.8 4.0 %collective-permute-start.5 = (f32[2,5,8,128]{3,2,1,0:T(8,128)S(1)}, f32[2,5,8,128]{3,2,1,0:T(8,128)S(1)}, u32[]{:S(2)}, u32[]{:S(2)}) collective-permute-start(f32[2,5,8,128]{3,2,1,0:T(8,128)S(1)} %get-tuple-element.34), channel_id=1, source_target_pairs={{0,56},{1,57},{2,58},{3,59},{4,60},{5,61},{6,62},{7,63},{8,0},{9,1... | collective-permute-start | bytes 122888 | tf_op jit(solution)/shard_map/ppermute | solution.py:402
  44.9 5.2 %collective-permute-start.4 = (f32[2,5,8,128]{3,2,1,0:T(8,128)S(1)}, f32[2,5,8,128]{3,2,1,0:T(8,128)S(1)}, u32[]{:S(2)}, u32[]{:S(2)}) collective-permute-start(f32[2,5,8,128]{3,2,1,0:T(8,128)S(1)} %get-tuple-element.33.own), channel_id=1, source_target_pairs={{0,8},{1,9},{2,10},{3,11},{4,12},{5,13},{6,14},{7,15},{8,16},{9,17... | collective-permute-start | bytes 122888 | tf_op jit(solution)/shard_map/ppermute | solution.py:401
  51.7 4.2 %collective-permute-start.7 = (f32[2,5,8,128]{3,2,1,0:T(8,128)S(1)}, f32[2,5,8,128]{3,2,1,0:T(8,128)S(1)}, u32[]{:S(2)}, u32[]{:S(2)}) collective-permute-start(f32[2,5,8,128]{3,2,1,0:T(8,128)S(1)} %get-tuple-element.37), channel_id=1, source_target_pairs={{0,56},{1,57},{2,58},{3,59},{4,60},{5,61},{6,62},{7,63},{8,0},{9,1... | collective-permute-start | bytes 122888 | tf_op jit(solution)/shard_map/ppermute | solution.py:402
  51.9 5.6 %collective-permute-start.6 = (f32[2,5,8,128]{3,2,1,0:T(8,128)S(1)}, f32[2,5,8,128]{3,2,1,0:T(8,128)S(1)}, u32[]{:S(2)}, u32[]{:S(2)}) collective-permute-start(f32[2,5,8,128]{3,2,1,0:T(8,128)S(1)} %get-tuple-element.36.own), channel_id=1, source_target_pairs={{0,8},{1,9},{2,10},{3,11},{4,12},{5,13},{6,14},{7,15},{8,16},{9,17... | collective-permute-start | bytes 122888 | tf_op jit(solution)/shard_map/ppermute | solution.py:401
  59.1 4.0 %collective-permute-start.9 = (f32[2,5,8,128]{3,2,1,0:T(8,128)S(1)}, f32[2,5,8,128]{3,2,1,0:T(8,128)S(1)}, u32[]{:S(2)}, u32[]{:S(2)}) collective-permute-start(f32[2,5,8,128]{3,2,1,0:T(8,128)S(1)} %get-tuple-element.40), channel_id=1, source_target_pairs={{0,56},{1,57},{2,58},{3,59},{4,60},{5,61},{6,62},{7,63},{8,0},{9,1... | collective-permute-start | bytes 122888 | tf_op jit(solution)/shard_map/ppermute | solution.py:402
  59.1 5.3 %collective-permute-start.8 = (f32[2,5,8,128]{3,2,1,0:T(8,128)S(1)}, f32[2,5,8,128]{3,2,1,0:T(8,128)S(1)}, u32[]{:S(2)}, u32[]{:S(2)}) collective-permute-start(f32[2,5,8,128]{3,2,1,0:T(8,128)S(1)} %get-tuple-element.39.own), channel_id=1, source_target_pairs={{0,8},{1,9},{2,10},{3,11},{4,12},{5,13},{6,14},{7,15},{8,16},{9,17... | collective-permute-start | bytes 122888 | tf_op jit(solution)/shard_map/ppermute | solution.py:401
  88.3 1.3 %collective-permute-start.10 = (f32[2,16,128]{2,1,0:T(8,128)S(1)}, f32[2,16,128]{2,1,0:T(8,128)S(1)}, u32[]{:S(2)}, u32[]{:S(2)}) collective-permute-start(f32[2,16,128]{2,1,0:T(8,128)S(1)} %get-tuple-element.42), channel_id=1, source_target_pairs={{0,64},{64,0},{128,192},{192,128},{1,65},{65,1},{129,193},{193,129... | collective-permute-start | bytes 49160 | tf_op jit(solution)/shard_map/ppermute | solution.py:439
  89.6 3.7 %collective-permute-start.11 = (f32[16,128]{1,0:T(8,128)S(1)}, f32[16,128]{1,0:T(8,128)S(1)}, u32[]{:S(2)}, u32[]{:S(2)}) collective-permute-start(f32[16,128]{1,0:T(8,128)S(1)} %slice_bitcast_fusion), channel_id=1, source_target_pairs={{0,128},{64,192},{128,0},{192,64},{1,129},{65,193},{129,1},{193,65... | collective-permute-start | bytes 24584 | tf_op jit(solution)/shard_map/ppermute | solution.py:440

commit v2 on v1

--- a/solution.py
+++ b/solution.py
@@ -10,6 +10,7 @@
 RADIUS = 4
 DEGREE = 4
 WINDOW = 17
+BATCH = 4
 
 stencil_weights = (-205.0 / 72.0, 1.6, -0.2, 8.0 / 315.0, -1.0 / 560.0)
 filter_centre = 10.0
@@ -70,18 +71,18 @@
         return n + (entry >= 0).astype(jnp.int32)
 
     count = lax.fori_loop(0, atoms, pick, jnp.int32(0), unroll=16)
-    table[0, count] = atoms * 256
-    pairs = (count + 1) >> 1
-    table[1, 0] = pairs
+    for i in range(BATCH - 1):
+        table[0, count + i] = atoms * 256
+    batches = (count + BATCH - 1) // BATCH
+    table[1, 0] = batches
     table[1, 1] = info[1, 1]
-    table[1, 2] = info[1, 2]
     for c in loads:
         c.wait()
     sub = lax.broadcasted_iota(jnp.int32, (WINDOW * 8, points), 0)
     lane = lax.broadcasted_iota(jnp.int32, (128, points), 0)
 
-    def pair(m, carry):
-        for n in (2 * m, 2 * m + 1):
+    def batch(m, carry):
+        for n in [BATCH * m + i for i in range(BATCH)]:
             entry = table[0, n]
             a = jnp.minimum(entry >> 8, atoms - 1)
             rel = idx[pl.ds(a, 1), :] - (base + (entry & 255)) * cells
@@ -102,25 +103,25 @@
         return carry
 
     def store(m):
-        two = pl.ds(2 * m, 2)
-        return pltpu.make_async_copy(blocks.at[two], blocks_far.at[two], sems.at[2 + m])
+        some = pl.ds(BATCH * m, BATCH)
+        return pltpu.make_async_copy(blocks.at[some], blocks_far.at[some], sems.at[2 + m])
 
     def stored(m, carry):
         store(m).wait()
         return carry
 
-    lax.fori_loop(0, pairs, pair, 0)
-    lax.fori_loop(0, pairs, stored, 0)
+    lax.fori_loop(0, batches, batch, 0)
+    lax.fori_loop(0, batches, stored, 0)
 
 
 def coefficients(table, field, blocks, sums, ready=None):
     atoms = blocks.shape[0]
     sums[...] = jnp.zeros_like(sums)
 
-    def pair(m, carry):
+    def batch(m, carry):
         if ready is not None:
             ready(m)
-        for n in (2 * m, 2 * m + 1):
+        for n in [BATCH * m + i for i in range(BATCH)]:
             entry = table[0, n]
             b = blocks[n]
             for s in range(2):
@@ -128,7 +129,7 @@
                 sums[s, pl.ds(entry >> 8, 1), :] = jnp.sum(jnp.sum(b * v, axis=0), axis=0, keepdims=True)
         return carry
 
-    lax.fori_loop(0, table[1, 0], pair, 0)
+    lax.fori_loop(0, table[1, 0], batch, 0)
     ones = jnp.ones((8, 128), jnp.float32)
     return [
         lax.dot_general(
@@ -149,8 +150,8 @@
 
 def first_kernel(table, got, blocks_far, y, up, down, blocks, sums, sems):
     def load(m):
-        two = pl.ds(2 * m, 2)
-        return pltpu.make_async_copy(blocks_far.at[two], blocks.at[two], sems.at[m])
+        some = pl.ds(BATCH * m, BATCH)
+        return pltpu.make_async_copy(blocks_far.at[some], blocks.at[some], sems.at[m])
 
     def begin(m, carry):
         load(m).start()
@@ -256,7 +257,7 @@
                 new[s, p] = new[s, p] + acc
 
     def spread(m, carry):
-        for n in (2 * m, 2 * m + 1):
+        for n in [BATCH * m + i for i in range(BATCH)]:
             entry = table[0, n]
             b = blocks[n]
             window = pl.ds(entry & 255, WINDOW)
@@ -279,7 +280,7 @@
         fill_messages(new, coefficients(table, new, blocks, sums), up, down)
 
 
-def product_kernel(table, got, keep, give, rows):
+def product_kernel(got, rows):
     states = rows.shape[0]
     total = None
     for r in range(0, 16, 2):
@@ -292,12 +293,6 @@
         )
         total = term if total is None else total + term
     rows[...] = jnp.concatenate([total[0:states], total[states : 2 * states]], axis=1)
-    band = table[1, 2]
-    size = keep.shape[1]
-    for other in range(2):
-        chip = band ^ (2 * other)
-        keep[other] = rows[pl.ds(pl.multiple_of(chip * size, size), size), :]
-        give[other] = rows[pl.ds(pl.multiple_of((chip ^ 1) * size, size), size), :]
 
 
 def pack_kernel(y, parts, out):
@@ -361,9 +356,7 @@
     high = jnp.max(support, axis=1) - place * planes
     entry = jnp.arange(atoms, dtype=jnp.int32) * 256 + jnp.clip(low, 0, planes - WINDOW)
     entry = jnp.where((high >= 0) & (low < planes), entry, -1)
-    lane = jnp.arange(atoms, dtype=jnp.int32)
-    where = jnp.where(lane == 1, place, jnp.where(lane == 2, lax.axis_index("band"), 0))
-    info = jnp.stack([entry, where]).astype(jnp.int32)
+    info = jnp.stack([entry, jnp.full((atoms,), place)]).astype(jnp.int32)
 
     field = shape((per, planes, ny, nz), f32)
     message = shape((per, 5, ny, nz), f32)
@@ -383,7 +376,7 @@
             pltpu.VMEM(proj_index.shape, jnp.int32),
             pltpu.VMEM(proj_value.shape, f32),
             pltpu.VMEM(block, f32),
-            pltpu.SemaphoreType.DMA((2 + atoms // 2,)),
+            pltpu.SemaphoreType.DMA((2 + atoms // BATCH,)),
         ],
         vmem=16,
     )(info, far(proj_index), far(proj_value))
@@ -393,7 +386,7 @@
         (field, message, message, shape(block, f32)),
         [SMEM, VMEM, HBM],
         (VMEM,) * 4,
-        [sums, pltpu.SemaphoreType.DMA((atoms // 2,))],
+        [sums, pltpu.SemaphoreType.DMA((atoms // BATCH,))],
         vmem=16,
     )(table, start, far(blocks_far))
 
@@ -432,12 +425,14 @@
         [new, sums],
     )(table, local("image", current, start), blocks, strength, below, above, up, current)
     got = lax.all_to_all(send, ("band", "grid"), 0, 0, axis_index_groups=whole_plane, tiled=True)
-    half = shape((2, count, 2 * everyone), f32)
-    keep, give = call(
-        product_kernel, "product", (half, half), [SMEM, VMEM], (VMEM, VMEM), [pltpu.VMEM((everyone, 2 * everyone), f32)]
-    )(table, got.reshape(everyone * 32, nz))
-    keep = keep + lax.ppermute(give, "band", [(i, i ^ 1) for i in range(bands)])
-    rows = keep[0] + lax.ppermute(keep[1], "band", [(i, i ^ 2) for i in range(bands)])
+    part = call(product_kernel, "product", shape((everyone, 2 * everyone), f32), [VMEM], VMEM)(
+        got.reshape(everyone * 32, nz)
+    )
+    band = lax.axis_index("band")
+    part = part + lax.ppermute(part, "band", [(i, i ^ 1) for i in range(bands)])
+    mine = lax.dynamic_slice_in_dim(part, band * count, count, axis=0)
+    other = lax.dynamic_slice_in_dim(part, (band ^ 2) * count, count, axis=0)
+    rows = mine + lax.ppermute(other, "band", [(i, i ^ 2) for i in range(bands)])
 
     copies = jnp.broadcast_to(rows, (zs, *rows.shape))
     copies = lax.all_to_all(copies, "grid", 0, 0, axis_index_groups=along_z, tiled=True)

time: 123 us -> 120 us (0.976)
  waiting for transfers between devices: 20 us -> 14.1 us
  starting transfers between devices: 21.7 us -> 26.6 us
    ppermute x5, waiting for transfers between devices: 8.82 us -> 1.29 us  [exchange(): lax.ppermute(up, 'grid', [(i, (i + group) % grid) for i in range(grid)])]
    ppermute x5, starting transfers between devices: 6.27 us -> 11.1 us  [exchange(): lax.ppermute(down, 'grid', [(i, (i - group) % grid) for i in range(grid)])]
  transfers between devices with their start and end apart: 13 -> 13, of which waited for: 12 -> 11; matrix products, arithmetic and copies ran while one was open for 1% -> 1% of each run, Pallas kernels for 12% -> 12%
where the time goes in v2:
time: 120 us; the launch traced here: 119 us
  blocking collectives  47.8 us (40%)
  Pallas kernels  29.1 us (24%)
  starting transfers between devices  26.6 us (22%)
  waiting for transfers between devices  14.1 us (12%)
    all_to_all x1, blocking collectives, per_device(): lax.all_to_all(send, ('band', 'grid'), 0, 0, axis_index_groups=whole_plan...  20.8 us
    all_to_all x1, blocking collectives, per_device(): lax.all_to_all(packed, 'grid', 0, 0, axis_index_groups=in_plane, tiled=True)  14.3 us
    all_to_all x1, blocking collectives, per_device(): lax.all_to_all(copies, 'grid', 0, 0, axis_index_groups=along_z, tiled=True)  12.6 us
    ppermute x5, starting transfers between devices, exchange(): lax.ppermute(down, 'grid', [(i, (i - group) % grid) for i in range(grid)])  11.1 us
    pallas_call x5, Pallas kernels, local(): call(functools.partial(stencil_kernel, mode), 'stencil', field, [VMEM] *...  8.46 us
    ppermute x5, starting transfers between devices, exchange(): lax.ppermute(up, 'grid', [(i, (i + group) % grid) for i in range(grid)])  7.87 us
    pallas_call x4, Pallas kernels, per_device(): call(functools.partial(finish_kernel, mode), 'finish', (field, message, m...  7.07 us
    all_to_all x1, waiting for transfers between devices, per_device(): lax.all_to_all(parcel, 'grid', 0, 0, axis_index_groups=in_plane, tiled=True)  6.96 us
  transfers between devices with their start and end apart: 13, of which 11 were waited for; matrix products, arithmetic and copies ran while one was open for 1% of the time, Pallas kernels for 12%

profile of v2, /device:TPU:2, one launch (start us, length us, event | category | flops | bytes accessed | tf_op | source)
XLA Modules:
  0.0 119.4 jit_solution(10594943949883391347)
XLA Ops:
  0.6 2.0 %parcel.1 = f32[8,3,8,8,128]{4,3,2,1,0:T(8,128)} custom-call(f32[8,2,8,8,128]{4,3,2,1,0:T(8,128)} %bitcast.15, f32[8,8,128]{2,1,0:T(8,128)} %potential.1), custom_call_target="tpu_custom_call" | custom-call | flops 4000000 | bytes 2000000 | tf_op jit(solution)/shard_map/parcel/pallas_call | solution.py:339
  2.6 6.0 %all-to-all-start = ((f32[8,3,8,8,128]{4,3,2,1,0:T(8,128)}), f32[8,3,8,8,128]{4,3,2,1,0:T(8,128)S(1)}, u32[]{:S(2)}, u32[]{:S(2)}) async-start(f32[8,3,8,8,128]{4,3,2,1,0:T(8,128)} %parcel.1), calls=%async_computation | async-start | bytes 1572864 | tf_op jit(solution)/shard_map/all_to_all | solution.py:351
  8.7 0.9 shift-right-arithmetic_reduce_fusion.1
  9.7 5.4 %build.1 = (f32[128,17,8,128]{3,2,1,0:T(8,128)}, s32[2,256]{1,0:T(2,128)S(1)}) custom-call(s32[2,128]{1,0:T(2,128)S(1)} %stack.4.info, s32[128,128]{1,0:T(8,128)} %idx_far.1, f32[128,128]{1,0:T(8,128)} %val_far.1), custom_call_target="tpu_custom_call" | custom-call | flops 4000000 | bytes 2000000 | tf_op jit(solution)/shard_map/build/pallas_call | solution.py:369
  15.1 7.0 %all-to-all-done.got.refs_0_.refs_1_ = f32[8,3,8,8,128]{4,3,2,1,0:T(8,128)S(1)} async-done(((f32[8,3,8,8,128]{4,3,2,1,0:T(8,128)}), f32[8,3,8,8,128]{4,3,2,1,0:T(8,128)S(1)}, u32[]{:S(2)}, u32[]{:S(2)}) %all-to-all-start) | async-done | bytes 786464 | tf_op jit(solution)/shard_map/all_to_all | solution.py:351
  22.1 2.6 %first.1 = (f32[2,64,8,128]{3,2,1,0:T(8,128)S(1)}, f32[2,5,8,128]{3,2,1,0:T(8,128)S(1)}, f32[2,5,8,128]{3,2,1,0:T(8,128)S(1)}, f32[128,17,8,128]{3,2,1,0:T(8,128)S(1)}) custom-call(s32[2,256]{1,0:T(2,128)S(1)} %get-tuple-element.21.table, f32[8,3,8,8,128]{4,3,2,1,0:T(8,128)S(1)} %all-to-all-done.got.refs_0_.refs_1_, ...), custom_call_target="tpu_custom_call" | custom-call | flops 4000000 | bytes 2000000 | tf_op jit(solution)/shard_map/first/pallas_call | solution.py:383
  24.7 2.0 %collective-permute-start = (f32[2,5,8,128]{3,2,1,0:T(8,128)S(1)}, f32[2,5,8,128]{3,2,1,0:T(8,128)S(1)}, u32[]{:S(2)}, u32[]{:S(2)}) collective-permute-start(f32[2,5,8,128]{3,2,1,0:T(8,128)S(1)} %get-tuple-element.25.own), channel_id=1, source_target_pairs={{0,8},{1,9},{2,10},{3,11},{4,12},{5,13},{6,14},{7,15},{8,16},{9,17... | collective-permute-start | bytes 122888 | tf_op jit(solution)/shard_map/ppermute | solution.py:394
  26.7 4.0 %collective-permute-start.1 = (f32[2,5,8,128]{3,2,1,0:T(8,128)S(1)}, f32[2,5,8,128]{3,2,1,0:T(8,128)S(1)}, u32[]{:S(2)}, u32[]{:S(2)}) collective-permute-start(f32[2,5,8,128]{3,2,1,0:T(8,128)S(1)} %get-tuple-element.26), channel_id=1, source_target_pairs={{0,56},{1,57},{2,58},{3,59},{4,60},{5,61},{6,62},{7,63},{8,0},{9,1... | collective-permute-start | bytes 122888 | tf_op jit(solution)/shard_map/ppermute | solution.py:395
  30.7 1.7 %stencil.5.partial = f32[2,64,8,128]{3,2,1,0:T(8,128)S(1)} custom-call(f32[2,64,8,128]{3,2,1,0:T(8,128)S(1)} %get-tuple-element.23.y.refs_0_, f32[8,3,8,8,128]{4,3,2,1,0:T(8,128)S(1)} %all-to-all-done.got.refs_0_.refs_1_), custom_call_target="tpu_custom_call" | custom-call | flops 4000000 | bytes 2000000 | tf_op jit(solution)/shard_map/stencil/pallas_call | solution.py:399
  32.6 1.8 %finish.4 = (f32[2,64,8,128]{3,2,1,0:T(8,128)S(1)}, f32[2,5,8,128]{3,2,1,0:T(8,128)S(1)}, f32[2,5,8,128]{3,2,1,0:T(8,128)S(1)}) custom-call(s32[2,256]{1,0:T(2,128)S(1)} %get-tuple-element.21.table, f32[2,64,8,128]{3,2,1,0:T(8,128)S(1)} %stencil.5.partial, f32[128,17,8,128]{3,2,1,0:T(8,128)S(1)} %get-tuple-element.24.blocks, f32[1,128]{1,0:T(1,128)S(1)} %bitcast.10, ...), custom_call_target="tpu_custom_call" | custom-call | flops 4000000 | bytes 2000000 | tf_op jit(solution)/shard_map/finish/pallas_call | solution.py:408
  34.3 3.3 %collective-permute-start.3 = (f32[2,5,8,128]{3,2,1,0:T(8,128)S(1)}, f32[2,5,8,128]{3,2,1,0:T(8,128)S(1)}, u32[]{:S(2)}, u32[]{:S(2)}) collective-permute-start(f32[2,5,8,128]{3,2,1,0:T(8,128)S(1)} %get-tuple-element.29), channel_id=1, source_target_pairs={{0,56},{1,57},{2,58},{3,59},{4,60},{5,61},{6,62},{7,63},{8,0},{9,1... | collective-permute-start | bytes 122888 | tf_op jit(solution)/shard_map/ppermute | solution.py:395
  37.6 1.7 %stencil.6.partial = f32[2,64,8,128]{3,2,1,0:T(8,128)S(1)} custom-call(f32[2,64,8,128]{3,2,1,0:T(8,128)S(1)} %get-tuple-element.27.y.refs_0_, f32[2,64,8,128]{3,2,1,0:T(8,128)S(1)} %get-tuple-element.23.y.refs_0_, f32[8,3,8,8,128]{4,3,2,1,0:T(8,128)S(1)} %all-to-all-done.got.refs_0_.refs_1_), custom_call_target="tpu_custom_call" | custom-call | flops 4000000 | bytes 2000000 | tf_op jit(solution)/shard_map/stencil/pallas_call | solution.py:399
  39.6 1.8 %finish.5 = (f32[2,64,8,128]{3,2,1,0:T(8,128)S(1)}, f32[2,5,8,128]{3,2,1,0:T(8,128)S(1)}, f32[2,5,8,128]{3,2,1,0:T(8,128)S(1)}) custom-call(s32[2,256]{1,0:T(2,128)S(1)} %get-tuple-element.21.table, f32[2,64,8,128]{3,2,1,0:T(8,128)S(1)} %stencil.6.partial, f32[128,17,8,128]{3,2,1,0:T(8,128)S(1)} %get-tuple-element.24.blocks, f32[1,128]{1,0:T(1,128)S(1)} %bitcast.11, ...), custom_call_target="tpu_custom_call" | custom-call | flops 4000000 | bytes 2000000 | tf_op jit(solution)/shard_map/finish/pallas_call | solution.py:408
  41.3 2.9 %collective-permute-start.4 = (f32[2,5,8,128]{3,2,1,0:T(8,128)S(1)}, f32[2,5,8,128]{3,2,1,0:T(8,128)S(1)}, u32[]{:S(2)}, u32[]{:S(2)}) collective-permute-start(f32[2,5,8,128]{3,2,1,0:T(8,128)S(1)} %get-tuple-element.31.own), channel_id=1, source_target_pairs={{0,8},{1,9},{2,10},{3,11},{4,12},{5,13},{6,14},{7,15},{8,16},{9,17... | collective-permute-start | bytes 122888 | tf_op jit(solution)/shard_map/ppermute | solution.py:394
  44.6 1.7 %stencil.7.partial = f32[2,64,8,128]{3,2,1,0:T(8,128)S(1)} custom-call(f32[2,64,8,128]{3,2,1,0:T(8,128)S(1)} %get-tuple-element.30.y.refs_0_, f32[2,64,8,128]{3,2,1,0:T(8,128)S(1)} %get-tuple-element.27.y.refs_0_, f32[8,3,8,8,128]{4,3,2,1,0:T(8,128)S(1)} %all-to-all-done.got.refs_0_.refs_1_), custom_call_target="tpu_custom_call" | custom-call | flops 4000000 | bytes 2000000 | tf_op jit(solution)/shard_map/stencil/pallas_call | solution.py:399
  46.6 1.9 %collective-permute-done.5.above = f32[2,5,8,128]{3,2,1,0:T(8,128)S(1)} collective-permute-done((f32[2,5,8,128]{3,2,1,0:T(8,128)S(1)}, f32[2,5,8,128]{3,2,1,0:T(8,128)S(1)}, u32[]{:S(2)}, u32[]{:S(2)}) %collective-permute-start.5) | collective-permute-done | bytes 40992 | tf_op jit(solution)/shard_map/ppermute | solution.py:395
  48.5 1.8 %finish.6 = (f32[2,64,8,128]{3,2,1,0:T(8,128)S(1)}, f32[2,5,8,128]{3,2,1,0:T(8,128)S(1)}, f32[2,5,8,128]{3,2,1,0:T(8,128)S(1)}) custom-call(s32[2,256]{1,0:T(2,128)S(1)} %get-tuple-element.21.table, f32[2,64,8,128]{3,2,1,0:T(8,128)S(1)} %stencil.7.partial, f32[128,17,8,128]{3,2,1,0:T(8,128)S(1)} %get-tuple-element.24.blocks, f32[1,128]{1,0:T(1,128)S(1)} %bitcast.12, ...), custom_call_target="tpu_custom_call" | custom-call | flops 4000000 | bytes 2000000 | tf_op jit(solution)/shard_map/finish/pallas_call | solution.py:408
  50.2 1.7 %collective-permute-start.6 = (f32[2,5,8,128]{3,2,1,0:T(8,128)S(1)}, f32[2,5,8,128]{3,2,1,0:T(8,128)S(1)}, u32[]{:S(2)}, u32[]{:S(2)}) collective-permute-start(f32[2,5,8,128]{3,2,1,0:T(8,128)S(1)} %get-tuple-element.34.own), channel_id=1, source_target_pairs={{0,8},{1,9},{2,10},{3,11},{4,12},{5,13},{6,14},{7,15},{8,16},{9,17... | collective-permute-start | bytes 122888 | tf_op jit(solution)/shard_map/ppermute | solution.py:394
  52.0 1.5 %collective-permute-start.7 = (f32[2,5,8,128]{3,2,1,0:T(8,128)S(1)}, f32[2,5,8,128]{3,2,1,0:T(8,128)S(1)}, u32[]{:S(2)}, u32[]{:S(2)}) collective-permute-start(f32[2,5,8,128]{3,2,1,0:T(8,128)S(1)} %get-tuple-element.35), channel_id=1, source_target_pairs={{0,56},{1,57},{2,58},{3,59},{4,60},{5,61},{6,62},{7,63},{8,0},{9,1... | collective-permute-start | bytes 122888 | tf_op jit(solution)/shard_map/ppermute | solution.py:395
  53.5 1.7 %stencil.8.partial = f32[2,64,8,128]{3,2,1,0:T(8,128)S(1)} custom-call(f32[2,64,8,128]{3,2,1,0:T(8,128)S(1)} %get-tuple-element.33.y, f32[2,64,8,128]{3,2,1,0:T(8,128)S(1)} %get-tuple-element.30.y.refs_0_, f32[8,3,8,8,128]{4,3,2,1,0:T(8,128)S(1)} %all-to-all-done.got.refs_0_.refs_1_), custom_call_target="tpu_custom_call" | custom-call | flops 4000000 | bytes 2000000 | tf_op jit(solution)/shard_map/stencil/pallas_call | solution.py:399
  56.0 1.8 %finish.7 = (f32[2,64,8,128]{3,2,1,0:T(8,128)S(1)}, f32[2,5,8,128]{3,2,1,0:T(8,128)S(1)}, f32[2,5,8,128]{3,2,1,0:T(8,128)S(1)}) custom-call(s32[2,256]{1,0:T(2,128)S(1)} %get-tuple-element.21.table, f32[2,64,8,128]{3,2,1,0:T(8,128)S(1)} %stencil.8.partial, f32[128,17,8,128]{3,2,1,0:T(8,128)S(1)} %get-tuple-element.24.blocks, f32[1,128]{1,0:T(1,128)S(1)} %bitcast.13, ...), custom_call_target="tpu_custom_call" | custom-call | flops 4000000 | bytes 2000000 | tf_op jit(solution)/shard_map/finish/pallas_call | solution.py:408
  57.7 1.3 %collective-permute-start.8 = (f32[2,5,8,128]{3,2,1,0:T(8,128)S(1)}, f32[2,5,8,128]{3,2,1,0:T(8,128)S(1)}, u32[]{:S(2)}, u32[]{:S(2)}) collective-permute-start(f32[2,5,8,128]{3,2,1,0:T(8,128)S(1)} %get-tuple-element.37.own), channel_id=1, source_target_pairs={{0,8},{1,9},{2,10},{3,11},{4,12},{5,13},{6,14},{7,15},{8,16},{9,17... | collective-permute-start | bytes 122888 | tf_op jit(solution)/shard_map/ppermute | solution.py:394
  59.0 2.0 %collective-permute-start.9 = (f32[2,5,8,128]{3,2,1,0:T(8,128)S(1)}, f32[2,5,8,128]{3,2,1,0:T(8,128)S(1)}, u32[]{:S(2)}, u32[]{:S(2)}) collective-permute-start(f32[2,5,8,128]{3,2,1,0:T(8,128)S(1)} %get-tuple-element.38), channel_id=1, source_target_pairs={{0,56},{1,57},{2,58},{3,59},{4,60},{5,61},{6,62},{7,63},{8,0},{9,1... | collective-permute-start | bytes 122888 | tf_op jit(solution)/shard_map/ppermute | solution.py:395
  61.0 1.7 %stencil.9.partial = f32[2,64,8,128]{3,2,1,0:T(8,128)S(1)} custom-call(f32[2,64,8,128]{3,2,1,0:T(8,128)S(1)} %get-tuple-element.36.y.refs_0_, f32[8,3,8,8,128]{4,3,2,1,0:T(8,128)S(1)} %all-to-all-done.got.refs_0_.refs_1_), custom_call_target="tpu_custom_call" | custom-call | flops 4000000 | bytes 2000000 | tf_op jit(solution)/shard_map/stencil/pallas_call | solution.py:399
  63.0 1.1 image.1
  64.1 20.8 %all_to_all.20 = f32[32,2,2,16,128]{4,3,2,1,0:T(8,128)S(1)} all-to-all(f32[32,2,2,16,128]{4,3,2,1,0:T(8,128)S(1)} %image.1), channel_id=1, replica_groups={{0,1,2,3,4,5,6,7,64,65,66,67,68,69,70,71,128,129,130,131,132,133,134,13..., dimensions={0} | all-to-all | bytes 2097152 | tf_op jit(solution)/shard_map/all_to_all | solution.py:427
  85.0 1.5 %product.1 = f32[64,128]{1,0:T(8,128)S(1)} custom-call(f32[2048,128]{1,0:T(8,128)S(1)} %bitcast.9), custom_call_target="tpu_custom_call" | custom-call | flops 4000000 | bytes 2000000 | tf_op jit(solution)/shard_map/product/pallas_call | solution.py:428
  86.6 1.2 collective-permute-done.10
  87.8 1.5 %collective-permute-start.11 = (f32[16,128]{1,0:T(8,128)S(1)}, f32[16,128]{1,0:T(8,128)S(1)}, u32[]{:S(2)}, u32[]{:S(2)}) collective-permute-start(f32[16,128]{1,0:T(8,128)S(1)} %constant_dynamic-slice_fusion), channel_id=1, source_target_pairs={{0,128},{64,192},{128,0},{192,64},{1,129},{65,193},{129,1},{193,65... | collective-permute-start | bytes 24584 | tf_op jit(solution)/shard_map/ppermute | solution.py:435
  89.3 2.2 %collective-permute-done.11 = f32[16,128]{1,0:T(8,128)S(1)} collective-permute-done((f32[16,128]{1,0:T(8,128)S(1)}, f32[16,128]{1,0:T(8,128)S(1)}, u32[]{:S(2)}, u32[]{:S(2)}) %collective-permute-start.11) | collective-permute-done | bytes 8224 | tf_op jit(solution)/shard_map/ppermute | solution.py:435
  91.6 12.6 %all_to_all.21.parts = f32[8,16,128]{2,1,0:T(8,128)S(1)} all-to-all(f32[8,16,128]{2,1,0:T(8,128)S(1)} %broadcast_in_dim.8), channel_id=1, replica_groups={{0,8,16,24,32,40,48,56},{1,9,17,25,33,41,49,57},{2,10,18,26,34,42,50,58..., dimensions={0} | all-to-all | bytes 131072 | tf_op jit(solution)/shard_map/all_to_all | solution.py:438
  104.2 14.3 %all_to_all.22.got = f32[8,18,8,128]{3,2,1,0:T(8,128)S(1)} all-to-all(f32[8,18,8,128]{3,2,1,0:T(8,128)S(1)} %pack.1), channel_id=1, replica_groups={{0,1,2,3,4,5,6,7},{8,9,10,11,12,13,14,15},{16,17,18,19,20,21,22,23},{24..., dimensions={0} | all-to-all | bytes 1179648 | tf_op jit(solution)/shard_map/all_to_all | solution.py:440
  (22 shorter events, 3.2 us)
Async XLA Ops:
  0.6 31.9 %copy-start = (f32[128]{0:T(128)S(1)}, f32[128]{0:T(128)}, u32[]{:S(2)}) copy-start(f32[128]{0:T(128)} %param.9) | copy-start | bytes 1540
  2.6 19.4 %all-to-all-start = ((f32[8,3,8,8,128]{4,3,2,1,0:T(8,128)}), f32[8,3,8,8,128]{4,3,2,1,0:T(8,128)S(1)}, u32[]{:S(2)}, u32[]{:S(2)}) async-start(f32[8,3,8,8,128]{4,3,2,1,0:T(8,128)} %parcel.1), calls=%async_computation | async-start | bytes 1572864 | tf_op jit(solution)/shard_map/all_to_all | solution.py:351
  24.7 7.8 %collective-permute-start = (f32[2,5,8,128]{3,2,1,0:T(8,128)S(1)}, f32[2,5,8,128]{3,2,1,0:T(8,128)S(1)}, u32[]{:S(2)}, u32[]{:S(2)}) collective-permute-start(f32[2,5,8,128]{3,2,1,0:T(8,128)S(1)} %get-tuple-element.25.own), channel_id=1, source_target_pairs={{0,8},{1,9},{2,10},{3,11},{4,12},{5,13},{6,14},{7,15},{8,16},{9,17... | collective-permute-start | bytes 122888 | tf_op jit(solution)/shard_map/ppermute | solution.py:394
  26.7 5.8 %collective-permute-start.1 = (f32[2,5,8,128]{3,2,1,0:T(8,128)S(1)}, f32[2,5,8,128]{3,2,1,0:T(8,128)S(1)}, u32[]{:S(2)}, u32[]{:S(2)}) collective-permute-start(f32[2,5,8,128]{3,2,1,0:T(8,128)S(1)} %get-tuple-element.26), channel_id=1, source_target_pairs={{0,56},{1,57},{2,58},{3,59},{4,60},{5,61},{6,62},{7,63},{8,0},{9,1... | collective-permute-start | bytes 122888 | tf_op jit(solution)/shard_map/ppermute | solution.py:395
  34.3 5.2 %collective-permute-start.2 = (f32[2,5,8,128]{3,2,1,0:T(8,128)S(1)}, f32[2,5,8,128]{3,2,1,0:T(8,128)S(1)}, u32[]{:S(2)}, u32[]{:S(2)}) collective-permute-start(f32[2,5,8,128]{3,2,1,0:T(8,128)S(1)} %get-tuple-element.28.own), channel_id=1, source_target_pairs={{0,8},{1,9},{2,10},{3,11},{4,12},{5,13},{6,14},{7,15},{8,16},{9,17... | collective-permute-start | bytes 122888 | tf_op jit(solution)/shard_map/ppermute | solution.py:394
  34.3 5.2 %collective-permute-start.3 = (f32[2,5,8,128]{3,2,1,0:T(8,128)S(1)}, f32[2,5,8,128]{3,2,1,0:T(8,128)S(1)}, u32[]{:S(2)}, u32[]{:S(2)}) collective-permute-start(f32[2,5,8,128]{3,2,1,0:T(8,128)S(1)} %get-tuple-element.29), channel_id=1, source_target_pairs={{0,56},{1,57},{2,58},{3,59},{4,60},{5,61},{6,62},{7,63},{8,0},{9,1... | collective-permute-start | bytes 122888 | tf_op jit(solution)/shard_map/ppermute | solution.py:395
  41.3 5.2 %collective-permute-start.4 = (f32[2,5,8,128]{3,2,1,0:T(8,128)S(1)}, f32[2,5,8,128]{3,2,1,0:T(8,128)S(1)}, u32[]{:S(2)}, u32[]{:S(2)}) collective-permute-start(f32[2,5,8,128]{3,2,1,0:T(8,128)S(1)} %get-tuple-element.31.own), channel_id=1, source_target_pairs={{0,8},{1,9},{2,10},{3,11},{4,12},{5,13},{6,14},{7,15},{8,16},{9,17... | collective-permute-start | bytes 122888 | tf_op jit(solution)/shard_map/ppermute | solution.py:394
  44.2 4.3 %collective-permute-start.5 = (f32[2,5,8,128]{3,2,1,0:T(8,128)S(1)}, f32[2,5,8,128]{3,2,1,0:T(8,128)S(1)}, u32[]{:S(2)}, u32[]{:S(2)}) collective-permute-start(f32[2,5,8,128]{3,2,1,0:T(8,128)S(1)} %get-tuple-element.32), channel_id=1, source_target_pairs={{0,56},{1,57},{2,58},{3,59},{4,60},{5,61},{6,62},{7,63},{8,0},{9,1... | collective-permute-start | bytes 122888 | tf_op jit(solution)/shard_map/ppermute | solution.py:395
  50.2 5.2 %collective-permute-start.6 = (f32[2,5,8,128]{3,2,1,0:T(8,128)S(1)}, f32[2,5,8,128]{3,2,1,0:T(8,128)S(1)}, u32[]{:S(2)}, u32[]{:S(2)}) collective-permute-start(f32[2,5,8,128]{3,2,1,0:T(8,128)S(1)} %get-tuple-element.34.own), channel_id=1, source_target_pairs={{0,8},{1,9},{2,10},{3,11},{4,12},{5,13},{6,14},{7,15},{8,16},{9,17... | collective-permute-start | bytes 122888 | tf_op jit(solution)/shard_map/ppermute | solution.py:394
  52.0 4.0 %collective-permute-start.7 = (f32[2,5,8,128]{3,2,1,0:T(8,128)S(1)}, f32[2,5,8,128]{3,2,1,0:T(8,128)S(1)}, u32[]{:S(2)}, u32[]{:S(2)}) collective-permute-start(f32[2,5,8,128]{3,2,1,0:T(8,128)S(1)} %get-tuple-element.35), channel_id=1, source_target_pairs={{0,56},{1,57},{2,58},{3,59},{4,60},{5,61},{6,62},{7,63},{8,0},{9,1... | collective-permute-start | bytes 122888 | tf_op jit(solution)/shard_map/ppermute | solution.py:395
  57.7 5.2 %collective-permute-start.8 = (f32[2,5,8,128]{3,2,1,0:T(8,128)S(1)}, f32[2,5,8,128]{3,2,1,0:T(8,128)S(1)}, u32[]{:S(2)}, u32[]{:S(2)}) collective-permute-start(f32[2,5,8,128]{3,2,1,0:T(8,128)S(1)} %get-tuple-element.37.own), channel_id=1, source_target_pairs={{0,8},{1,9},{2,10},{3,11},{4,12},{5,13},{6,14},{7,15},{8,16},{9,17... | collective-permute-start | bytes 122888 | tf_op jit(solution)/shard_map/ppermute | solution.py:394
  59.0 4.0 %collective-permute-start.9 = (f32[2,5,8,128]{3,2,1,0:T(8,128)S(1)}, f32[2,5,8,128]{3,2,1,0:T(8,128)S(1)}, u32[]{:S(2)}, u32[]{:S(2)}) collective-permute-start(f32[2,5,8,128]{3,2,1,0:T(8,128)S(1)} %get-tuple-element.38), channel_id=1, source_target_pairs={{0,56},{1,57},{2,58},{3,59},{4,60},{5,61},{6,62},{7,63},{8,0},{9,1... | collective-permute-start | bytes 122888 | tf_op jit(solution)/shard_map/ppermute | solution.py:395
  86.5 1.3 %collective-permute-start.10 = (f32[64,128]{1,0:T(8,128)S(1)}, f32[64,128]{1,0:T(8,128)S(1)}, u32[]{:S(2)}, u32[]{:S(2)}) collective-permute-start(f32[64,128]{1,0:T(8,128)S(1)} %product.1), channel_id=1, source_target_pairs={{0,64},{64,0},{128,192},{192,128},{1,65},{65,1},{129,193},{193,129... | collective-permute-start | bytes 98312 | tf_op jit(solution)/shard_map/ppermute | solution.py:432
  87.8 3.7 %collective-permute-start.11 = (f32[16,128]{1,0:T(8,128)S(1)}, f32[16,128]{1,0:T(8,128)S(1)}, u32[]{:S(2)}, u32[]{:S(2)}) collective-permute-start(f32[16,128]{1,0:T(8,128)S(1)} %constant_dynamic-slice_fusion), channel_id=1, source_target_pairs={{0,128},{64,192},{128,0},{192,64},{1,129},{65,193},{129,1},{193,65... | collective-permute-start | bytes 24584 | tf_op jit(solution)/shard_map/ppermute | solution.py:435

commit v3 on v2

--- a/solution.py
+++ b/solution.py
@@ -369,7 +369,7 @@
     blocks_far, table = call(
         functools.partial(build_kernel, planes),
         "build",
-        (pltpu.HBM(block, f32), shape((2, 256), jnp.int32)),
+        (pltpu.HBM(block, f32), pltpu.SMEM((2, 256), jnp.int32)),
         [SMEM, HBM, HBM],
         (HBM, SMEM),
         [
@@ -380,6 +380,7 @@
         ],
         vmem=16,
     )(info, far(proj_index), far(proj_value))
+    table = pltpu.with_memory_space_constraint(table, pltpu.SMEM)
     current, up, down, blocks = call(
         first_kernel,
         "first",

time: 120 us -> 117 us (0.975)
  Pallas kernels: 29.1 us -> 25.2 us
    pallas_call x4, Pallas kernels: 7.07 us -> 4.85 us  [per_device(): call(functools.partial(finish_kernel, mode), 'finish', (field, message, m...]
  transfers between devices with their start and end apart: 13 -> 13, of which waited for: 11 -> 11; matrix products, arithmetic and copies ran while one was open for 1% -> 1% of each run, Pallas kernels for 12% -> 11%
where the time goes in v3:
time: 117 us; the launch traced here: 116 us
  blocking collectives  48.3 us (41%)
  starting transfers between devices  26.6 us (23%)
  Pallas kernels  25.2 us (22%)
  waiting for transfers between devices  14.6 us (12%)
    all_to_all x1, blocking collectives, per_device(): lax.all_to_all(send, ('band', 'grid'), 0, 0, axis_index_groups=whole_plan...  20.8 us
    all_to_all x1, blocking collectives, per_device(): lax.all_to_all(packed, 'grid', 0, 0, axis_index_groups=in_plane, tiled=True)  14.3 us
    all_to_all x1, blocking collectives, per_device(): lax.all_to_all(copies, 'grid', 0, 0, axis_index_groups=along_z, tiled=True)  13.2 us
    ppermute x5, starting transfers between devices, exchange(): lax.ppermute(down, 'grid', [(i, (i - group) % grid) for i in range(grid)])  11.2 us
    pallas_call x5, Pallas kernels, local(): call(functools.partial(stencil_kernel, mode), 'stencil', field, [VMEM] *...  8.46 us
    ppermute x5, starting transfers between devices, exchange(): lax.ppermute(up, 'grid', [(i, (i + group) % grid) for i in range(grid)])  7.77 us
    all_to_all x1, waiting for transfers between devices, per_device(): lax.all_to_all(parcel, 'grid', 0, 0, axis_index_groups=in_plane, tiled=True)  7.57 us
    all_to_all x1, starting transfers between devices, per_device(): lax.all_to_all(parcel, 'grid', 0, 0, axis_index_groups=in_plane, tiled=True)  6.04 us
  transfers between devices with their start and end apart: 13, of which 11 were waited for; matrix products, arithmetic and copies ran while one was open for 1% of the time, Pallas kernels for 11%

profile of v3, /device:TPU:2, one launch (start us, length us, event | category | flops | bytes accessed | tf_op | source)
XLA Modules:
  0.0 116.5 jit_solution(15844025807120158960)
XLA Ops:
  0.6 2.0 %parcel.1 = f32[8,3,8,8,128]{4,3,2,1,0:T(8,128)} custom-call(f32[8,2,8,8,128]{4,3,2,1,0:T(8,128)} %bitcast.15, f32[8,8,128]{2,1,0:T(8,128)} %potential.1), custom_call_target="tpu_custom_call" | custom-call | flops 4000000 | bytes 2000000 | tf_op jit(solution)/shard_map/parcel/pallas_call | solution.py:339
  2.6 6.0 %all-to-all-start = ((f32[8,3,8,8,128]{4,3,2,1,0:T(8,128)}), f32[8,3,8,8,128]{4,3,2,1,0:T(8,128)S(1)}, u32[]{:S(2)}, u32[]{:S(2)}) async-start(f32[8,3,8,8,128]{4,3,2,1,0:T(8,128)} %parcel.1), calls=%async_computation | async-start | bytes 1572864 | tf_op jit(solution)/shard_map/all_to_all | solution.py:351
  8.7 0.9 shift-right-arithmetic_reduce_fusion.1
  9.7 4.8 %build.1 = (f32[128,17,8,128]{3,2,1,0:T(8,128)}, s32[2,256]{1,0:T(2,128)S(4)}) custom-call(s32[2,128]{1,0:T(2,128)S(1)} %stack.4.info, s32[128,128]{1,0:T(8,128)} %idx_far.1, f32[128,128]{1,0:T(8,128)} %val_far.1), custom_call_target="tpu_custom_call" | custom-call | flops 4000000 | bytes 2000000 | tf_op jit(solution)/shard_map/build/pallas_call | solution.py:369
  14.5 7.6 %all-to-all-done.got.refs_0_.refs_1_ = f32[8,3,8,8,128]{4,3,2,1,0:T(8,128)S(1)} async-done(((f32[8,3,8,8,128]{4,3,2,1,0:T(8,128)}), f32[8,3,8,8,128]{4,3,2,1,0:T(8,128)S(1)}, u32[]{:S(2)}, u32[]{:S(2)}) %all-to-all-start) | async-done | bytes 786464 | tf_op jit(solution)/shard_map/all_to_all | solution.py:351
  22.1 2.0 %first.1 = (f32[2,64,8,128]{3,2,1,0:T(8,128)S(1)}, f32[2,5,8,128]{3,2,1,0:T(8,128)S(1)}, f32[2,5,8,128]{3,2,1,0:T(8,128)S(1)}, f32[128,17,8,128]{3,2,1,0:T(8,128)S(1)}) custom-call(s32[2,256]{1,0:T(2,128)S(4)} %get-tuple-element.21.table, f32[8,3,8,8,128]{4,3,2,1,0:T(8,128)S(1)} %all-to-all-done.got.refs_0_.refs_1_, ...), custom_call_target="tpu_custom_call" | custom-call | flops 4000000 | bytes 2000000 | tf_op jit(solution)/shard_map/first/pallas_call | solution.py:384
  24.1 1.8 %collective-permute-start = (f32[2,5,8,128]{3,2,1,0:T(8,128)S(1)}, f32[2,5,8,128]{3,2,1,0:T(8,128)S(1)}, u32[]{:S(2)}, u32[]{:S(2)}) collective-permute-start(f32[2,5,8,128]{3,2,1,0:T(8,128)S(1)} %get-tuple-element.25.own), channel_id=1, source_target_pairs={{0,8},{1,9},{2,10},{3,11},{4,12},{5,13},{6,14},{7,15},{8,16},{9,17... | collective-permute-start | bytes 122888 | tf_op jit(solution)/shard_map/ppermute | solution.py:395
  25.9 4.2 %collective-permute-start.1 = (f32[2,5,8,128]{3,2,1,0:T(8,128)S(1)}, f32[2,5,8,128]{3,2,1,0:T(8,128)S(1)}, u32[]{:S(2)}, u32[]{:S(2)}) collective-permute-start(f32[2,5,8,128]{3,2,1,0:T(8,128)S(1)} %get-tuple-element.26), channel_id=1, source_target_pairs={{0,56},{1,57},{2,58},{3,59},{4,60},{5,61},{6,62},{7,63},{8,0},{9,1... | collective-permute-start | bytes 122888 | tf_op jit(solution)/shard_map/ppermute | solution.py:396
  30.1 1.7 %stencil.5.partial = f32[2,64,8,128]{3,2,1,0:T(8,128)S(1)} custom-call(f32[2,64,8,128]{3,2,1,0:T(8,128)S(1)} %get-tuple-element.23.y.refs_0_, f32[8,3,8,8,128]{4,3,2,1,0:T(8,128)S(1)} %all-to-all-done.got.refs_0_.refs_1_), custom_call_target="tpu_custom_call" | custom-call | flops 4000000 | bytes 2000000 | tf_op jit(solution)/shard_map/stencil/pallas_call | solution.py:400
  32.0 1.2 %finish.4 = (f32[2,64,8,128]{3,2,1,0:T(8,128)S(1)}, f32[2,5,8,128]{3,2,1,0:T(8,128)S(1)}, f32[2,5,8,128]{3,2,1,0:T(8,128)S(1)}) custom-call(s32[2,256]{1,0:T(2,128)S(4)} %get-tuple-element.21.table, f32[2,64,8,128]{3,2,1,0:T(8,128)S(1)} %stencil.5.partial, f32[128,17,8,128]{3,2,1,0:T(8,128)S(1)} %get-tuple-element.24.blocks, f32[1,128]{1,0:T(1,128)S(1)} %bitcast.10, ...), custom_call_target="tpu_custom_call" | custom-call | flops 4000000 | bytes 2000000 | tf_op jit(solution)/shard_map/finish/pallas_call | solution.py:409
  33.2 3.3 %collective-permute-start.3 = (f32[2,5,8,128]{3,2,1,0:T(8,128)S(1)}, f32[2,5,8,128]{3,2,1,0:T(8,128)S(1)}, u32[]{:S(2)}, u32[]{:S(2)}) collective-permute-start(f32[2,5,8,128]{3,2,1,0:T(8,128)S(1)} %get-tuple-element.29), channel_id=1, source_target_pairs={{0,56},{1,57},{2,58},{3,59},{4,60},{5,61},{6,62},{7,63},{8,0},{9,1... | collective-permute-start | bytes 122888 | tf_op jit(solution)/shard_map/ppermute | solution.py:396
  36.4 1.7 %stencil.6.partial = f32[2,64,8,128]{3,2,1,0:T(8,128)S(1)} custom-call(f32[2,64,8,128]{3,2,1,0:T(8,128)S(1)} %get-tuple-element.27.y.refs_0_, f32[2,64,8,128]{3,2,1,0:T(8,128)S(1)} %get-tuple-element.23.y.refs_0_, f32[8,3,8,8,128]{4,3,2,1,0:T(8,128)S(1)} %all-to-all-done.got.refs_0_.refs_1_), custom_call_target="tpu_custom_call" | custom-call | flops 4000000 | bytes 2000000 | tf_op jit(solution)/shard_map/stencil/pallas_call | solution.py:400
  38.4 1.2 %finish.5 = (f32[2,64,8,128]{3,2,1,0:T(8,128)S(1)}, f32[2,5,8,128]{3,2,1,0:T(8,128)S(1)}, f32[2,5,8,128]{3,2,1,0:T(8,128)S(1)}) custom-call(s32[2,256]{1,0:T(2,128)S(4)} %get-tuple-element.21.table, f32[2,64,8,128]{3,2,1,0:T(8,128)S(1)} %stencil.6.partial, f32[128,17,8,128]{3,2,1,0:T(8,128)S(1)} %get-tuple-element.24.blocks, f32[1,128]{1,0:T(1,128)S(1)} %bitcast.11, ...), custom_call_target="tpu_custom_call" | custom-call | flops 4000000 | bytes 2000000 | tf_op jit(solution)/shard_map/finish/pallas_call | solution.py:409
  39.6 2.7 %collective-permute-start.4 = (f32[2,5,8,128]{3,2,1,0:T(8,128)S(1)}, f32[2,5,8,128]{3,2,1,0:T(8,128)S(1)}, u32[]{:S(2)}, u32[]{:S(2)}) collective-permute-start(f32[2,5,8,128]{3,2,1,0:T(8,128)S(1)} %get-tuple-element.31.own), channel_id=1, source_target_pairs={{0,8},{1,9},{2,10},{3,11},{4,12},{5,13},{6,14},{7,15},{8,16},{9,17... | collective-permute-start | bytes 122888 | tf_op jit(solution)/shard_map/ppermute | solution.py:395
  42.9 1.7 %stencil.7.partial = f32[2,64,8,128]{3,2,1,0:T(8,128)S(1)} custom-call(f32[2,64,8,128]{3,2,1,0:T(8,128)S(1)} %get-tuple-element.30.y.refs_0_, f32[2,64,8,128]{3,2,1,0:T(8,128)S(1)} %get-tuple-element.27.y.refs_0_, f32[8,3,8,8,128]{4,3,2,1,0:T(8,128)S(1)} %all-to-all-done.got.refs_0_.refs_1_), custom_call_target="tpu_custom_call" | custom-call | flops 4000000 | bytes 2000000 | tf_op jit(solution)/shard_map/stencil/pallas_call | solution.py:400
  44.9 1.5 %collective-permute-done.5.above = f32[2,5,8,128]{3,2,1,0:T(8,128)S(1)} collective-permute-done((f32[2,5,8,128]{3,2,1,0:T(8,128)S(1)}, f32[2,5,8,128]{3,2,1,0:T(8,128)S(1)}, u32[]{:S(2)}, u32[]{:S(2)}) %collective-permute-start.5) | collective-permute-done | bytes 40992 | tf_op jit(solution)/shard_map/ppermute | solution.py:396
  46.3 1.2 %finish.6 = (f32[2,64,8,128]{3,2,1,0:T(8,128)S(1)}, f32[2,5,8,128]{3,2,1,0:T(8,128)S(1)}, f32[2,5,8,128]{3,2,1,0:T(8,128)S(1)}) custom-call(s32[2,256]{1,0:T(2,128)S(4)} %get-tuple-element.21.table, f32[2,64,8,128]{3,2,1,0:T(8,128)S(1)} %stencil.7.partial, f32[128,17,8,128]{3,2,1,0:T(8,128)S(1)} %get-tuple-element.24.blocks, f32[1,128]{1,0:T(1,128)S(1)} %bitcast.12, ...), custom_call_target="tpu_custom_call" | custom-call | flops 4000000 | bytes 2000000 | tf_op jit(solution)/shard_map/finish/pallas_call | solution.py:409
  47.5 2.0 %collective-permute-start.6 = (f32[2,5,8,128]{3,2,1,0:T(8,128)S(1)}, f32[2,5,8,128]{3,2,1,0:T(8,128)S(1)}, u32[]{:S(2)}, u32[]{:S(2)}) collective-permute-start(f32[2,5,8,128]{3,2,1,0:T(8,128)S(1)} %get-tuple-element.34.own), channel_id=1, source_target_pairs={{0,8},{1,9},{2,10},{3,11},{4,12},{5,13},{6,14},{7,15},{8,16},{9,17... | collective-permute-start | bytes 122888 | tf_op jit(solution)/shard_map/ppermute | solution.py:395
  49.5 1.3 %collective-permute-start.7 = (f32[2,5,8,128]{3,2,1,0:T(8,128)S(1)}, f32[2,5,8,128]{3,2,1,0:T(8,128)S(1)}, u32[]{:S(2)}, u32[]{:S(2)}) collective-permute-start(f32[2,5,8,128]{3,2,1,0:T(8,128)S(1)} %get-tuple-element.35), channel_id=1, source_target_pairs={{0,56},{1,57},{2,58},{3,59},{4,60},{5,61},{6,62},{7,63},{8,0},{9,1... | collective-permute-start | bytes 122888 | tf_op jit(solution)/shard_map/ppermute | solution.py:396
  50.8 1.7 %stencil.8.partial = f32[2,64,8,128]{3,2,1,0:T(8,128)S(1)} custom-call(f32[2,64,8,128]{3,2,1,0:T(8,128)S(1)} %get-tuple-element.33.y, f32[2,64,8,128]{3,2,1,0:T(8,128)S(1)} %get-tuple-element.30.y.refs_0_, f32[8,3,8,8,128]{4,3,2,1,0:T(8,128)S(1)} %all-to-all-done.got.refs_0_.refs_1_), custom_call_target="tpu_custom_call" | custom-call | flops 4000000 | bytes 2000000 | tf_op jit(solution)/shard_map/stencil/pallas_call | solution.py:400
  53.5 1.2 %finish.7 = (f32[2,64,8,128]{3,2,1,0:T(8,128)S(1)}, f32[2,5,8,128]{3,2,1,0:T(8,128)S(1)}, f32[2,5,8,128]{3,2,1,0:T(8,128)S(1)}) custom-call(s32[2,256]{1,0:T(2,128)S(4)} %get-tuple-element.21.table, f32[2,64,8,128]{3,2,1,0:T(8,128)S(1)} %stencil.8.partial, f32[128,17,8,128]{3,2,1,0:T(8,128)S(1)} %get-tuple-element.24.blocks, f32[1,128]{1,0:T(1,128)S(1)} %bitcast.13, ...), custom_call_target="tpu_custom_call" | custom-call | flops 4000000 | bytes 2000000 | tf_op jit(solution)/shard_map/finish/pallas_call | solution.py:409
  54.7 1.4 %collective-permute-start.8 = (f32[2,5,8,128]{3,2,1,0:T(8,128)S(1)}, f32[2,5,8,128]{3,2,1,0:T(8,128)S(1)}, u32[]{:S(2)}, u32[]{:S(2)}) collective-permute-start(f32[2,5,8,128]{3,2,1,0:T(8,128)S(1)} %get-tuple-element.37.own), channel_id=1, source_target_pairs={{0,8},{1,9},{2,10},{3,11},{4,12},{5,13},{6,14},{7,15},{8,16},{9,17... | collective-permute-start | bytes 122888 | tf_op jit(solution)/shard_map/ppermute | solution.py:395
  56.1 1.9 %collective-permute-start.9 = (f32[2,5,8,128]{3,2,1,0:T(8,128)S(1)}, f32[2,5,8,128]{3,2,1,0:T(8,128)S(1)}, u32[]{:S(2)}, u32[]{:S(2)}) collective-permute-start(f32[2,5,8,128]{3,2,1,0:T(8,128)S(1)} %get-tuple-element.38), channel_id=1, source_target_pairs={{0,56},{1,57},{2,58},{3,59},{4,60},{5,61},{6,62},{7,63},{8,0},{9,1... | collective-permute-start | bytes 122888 | tf_op jit(solution)/shard_map/ppermute | solution.py:396
  58.0 1.7 %stencil.9.partial = f32[2,64,8,128]{3,2,1,0:T(8,128)S(1)} custom-call(f32[2,64,8,128]{3,2,1,0:T(8,128)S(1)} %get-tuple-element.36.y.refs_0_, f32[8,3,8,8,128]{4,3,2,1,0:T(8,128)S(1)} %all-to-all-done.got.refs_0_.refs_1_), custom_call_target="tpu_custom_call" | custom-call | flops 4000000 | bytes 2000000 | tf_op jit(solution)/shard_map/stencil/pallas_call | solution.py:400
  60.7 20.8 %all_to_all.20 = f32[32,2,2,16,128]{4,3,2,1,0:T(8,128)S(1)} all-to-all(f32[32,2,2,16,128]{4,3,2,1,0:T(8,128)S(1)} %image.1), channel_id=1, replica_groups={{0,1,2,3,4,5,6,7,64,65,66,67,68,69,70,71,128,129,130,131,132,133,134,13..., dimensions={0} | all-to-all | bytes 2097152 | tf_op jit(solution)/shard_map/all_to_all | solution.py:428
  81.5 1.5 %product.1 = f32[64,128]{1,0:T(8,128)S(1)} custom-call(f32[2048,128]{1,0:T(8,128)S(1)} %bitcast.9), custom_call_target="tpu_custom_call" | custom-call | flops 4000000 | bytes 2000000 | tf_op jit(solution)/shard_map/product/pallas_call | solution.py:429
  83.1 1.2 %collective-permute-done.10 = f32[64,128]{1,0:T(8,128)S(1)} collective-permute-done((f32[64,128]{1,0:T(8,128)S(1)}, f32[64,128]{1,0:T(8,128)S(1)}, u32[]{:S(2)}, u32[]{:S(2)}) %collective-permute-start.10) | collective-permute-done | bytes 32800 | tf_op jit(solution)/shard_map/ppermute | solution.py:433
  84.3 1.5 %collective-permute-start.11 = (f32[16,128]{1,0:T(8,128)S(1)}, f32[16,128]{1,0:T(8,128)S(1)}, u32[]{:S(2)}, u32[]{:S(2)}) collective-permute-start(f32[16,128]{1,0:T(8,128)S(1)} %constant_dynamic-slice_fusion), channel_id=1, source_target_pairs={{0,128},{64,192},{128,0},{192,64},{1,129},{65,193},{129,1},{193,65... | collective-permute-start | bytes 24584 | tf_op jit(solution)/shard_map/ppermute | solution.py:436
  85.8 2.2 %collective-permute-done.11 = f32[16,128]{1,0:T(8,128)S(1)} collective-permute-done((f32[16,128]{1,0:T(8,128)S(1)}, f32[16,128]{1,0:T(8,128)S(1)}, u32[]{:S(2)}, u32[]{:S(2)}) %collective-permute-start.11) | collective-permute-done | bytes 8224 | tf_op jit(solution)/shard_map/ppermute | solution.py:436
  88.0 13.2 %all_to_all.21.parts = f32[8,16,128]{2,1,0:T(8,128)S(1)} all-to-all(f32[8,16,128]{2,1,0:T(8,128)S(1)} %broadcast_in_dim.8), channel_id=1, replica_groups={{0,8,16,24,32,40,48,56},{1,9,17,25,33,41,49,57},{2,10,18,26,34,42,50,58..., dimensions={0} | all-to-all | bytes 131072 | tf_op jit(solution)/shard_map/all_to_all | solution.py:439
  101.3 14.3 %all_to_all.22.got = f32[8,18,8,128]{3,2,1,0:T(8,128)S(1)} all-to-all(f32[8,18,8,128]{3,2,1,0:T(8,128)S(1)} %pack.1), channel_id=1, replica_groups={{0,1,2,3,4,5,6,7},{8,9,10,11,12,13,14,15},{16,17,18,19,20,21,22,23},{24..., dimensions={0} | all-to-all | bytes 1179648 | tf_op jit(solution)/shard_map/all_to_all | solution.py:441
  115.7 0.8 unpack.1
  (22 shorter events, 3.5 us)
Async XLA Ops:
  0.6 31.3 %copy-start = (f32[128]{0:T(128)S(1)}, f32[128]{0:T(128)}, u32[]{:S(2)}) copy-start(f32[128]{0:T(128)} %param.9) | copy-start | bytes 1540
  2.6 19.4 %all-to-all-start = ((f32[8,3,8,8,128]{4,3,2,1,0:T(8,128)}), f32[8,3,8,8,128]{4,3,2,1,0:T(8,128)S(1)}, u32[]{:S(2)}, u32[]{:S(2)}) async-start(f32[8,3,8,8,128]{4,3,2,1,0:T(8,128)} %parcel.1), calls=%async_computation | async-start | bytes 1572864 | tf_op jit(solution)/shard_map/all_to_all | solution.py:351
  24.1 7.8 %collective-permute-start = (f32[2,5,8,128]{3,2,1,0:T(8,128)S(1)}, f32[2,5,8,128]{3,2,1,0:T(8,128)S(1)}, u32[]{:S(2)}, u32[]{:S(2)}) collective-permute-start(f32[2,5,8,128]{3,2,1,0:T(8,128)S(1)} %get-tuple-element.25.own), channel_id=1, source_target_pairs={{0,8},{1,9},{2,10},{3,11},{4,12},{5,13},{6,14},{7,15},{8,16},{9,17... | collective-permute-start | bytes 122888 | tf_op jit(solution)/shard_map/ppermute | solution.py:395
  25.9 6.1 %collective-permute-start.1 = (f32[2,5,8,128]{3,2,1,0:T(8,128)S(1)}, f32[2,5,8,128]{3,2,1,0:T(8,128)S(1)}, u32[]{:S(2)}, u32[]{:S(2)}) collective-permute-start(f32[2,5,8,128]{3,2,1,0:T(8,128)S(1)} %get-tuple-element.26), channel_id=1, source_target_pairs={{0,56},{1,57},{2,58},{3,59},{4,60},{5,61},{6,62},{7,63},{8,0},{9,1... | collective-permute-start | bytes 122888 | tf_op jit(solution)/shard_map/ppermute | solution.py:396
  33.2 5.2 %collective-permute-start.2 = (f32[2,5,8,128]{3,2,1,0:T(8,128)S(1)}, f32[2,5,8,128]{3,2,1,0:T(8,128)S(1)}, u32[]{:S(2)}, u32[]{:S(2)}) collective-permute-start(f32[2,5,8,128]{3,2,1,0:T(8,128)S(1)} %get-tuple-element.28.own), channel_id=1, source_target_pairs={{0,8},{1,9},{2,10},{3,11},{4,12},{5,13},{6,14},{7,15},{8,16},{9,17... | collective-permute-start | bytes 122888 | tf_op jit(solution)/shard_map/ppermute | solution.py:395
  33.2 5.2 %collective-permute-start.3 = (f32[2,5,8,128]{3,2,1,0:T(8,128)S(1)}, f32[2,5,8,128]{3,2,1,0:T(8,128)S(1)}, u32[]{:S(2)}, u32[]{:S(2)}) collective-permute-start(f32[2,5,8,128]{3,2,1,0:T(8,128)S(1)} %get-tuple-element.29), channel_id=1, source_target_pairs={{0,56},{1,57},{2,58},{3,59},{4,60},{5,61},{6,62},{7,63},{8,0},{9,1... | collective-permute-start | bytes 122888 | tf_op jit(solution)/shard_map/ppermute | solution.py:396
  39.6 5.2 %collective-permute-start.4 = (f32[2,5,8,128]{3,2,1,0:T(8,128)S(1)}, f32[2,5,8,128]{3,2,1,0:T(8,128)S(1)}, u32[]{:S(2)}, u32[]{:S(2)}) collective-permute-start(f32[2,5,8,128]{3,2,1,0:T(8,128)S(1)} %get-tuple-element.31.own), channel_id=1, source_target_pairs={{0,8},{1,9},{2,10},{3,11},{4,12},{5,13},{6,14},{7,15},{8,16},{9,17... | collective-permute-start | bytes 122888 | tf_op jit(solution)/shard_map/ppermute | solution.py:395
  42.3 4.0 %collective-permute-start.5 = (f32[2,5,8,128]{3,2,1,0:T(8,128)S(1)}, f32[2,5,8,128]{3,2,1,0:T(8,128)S(1)}, u32[]{:S(2)}, u32[]{:S(2)}) collective-permute-start(f32[2,5,8,128]{3,2,1,0:T(8,128)S(1)} %get-tuple-element.32), channel_id=1, source_target_pairs={{0,56},{1,57},{2,58},{3,59},{4,60},{5,61},{6,62},{7,63},{8,0},{9,1... | collective-permute-start | bytes 122888 | tf_op jit(solution)/shard_map/ppermute | solution.py:396
  47.5 5.2 %collective-permute-start.6 = (f32[2,5,8,128]{3,2,1,0:T(8,128)S(1)}, f32[2,5,8,128]{3,2,1,0:T(8,128)S(1)}, u32[]{:S(2)}, u32[]{:S(2)}) collective-permute-start(f32[2,5,8,128]{3,2,1,0:T(8,128)S(1)} %get-tuple-element.34.own), channel_id=1, source_target_pairs={{0,8},{1,9},{2,10},{3,11},{4,12},{5,13},{6,14},{7,15},{8,16},{9,17... | collective-permute-start | bytes 122888 | tf_op jit(solution)/shard_map/ppermute | solution.py:395
  49.5 4.0 %collective-permute-start.7 = (f32[2,5,8,128]{3,2,1,0:T(8,128)S(1)}, f32[2,5,8,128]{3,2,1,0:T(8,128)S(1)}, u32[]{:S(2)}, u32[]{:S(2)}) collective-permute-start(f32[2,5,8,128]{3,2,1,0:T(8,128)S(1)} %get-tuple-element.35), channel_id=1, source_target_pairs={{0,56},{1,57},{2,58},{3,59},{4,60},{5,61},{6,62},{7,63},{8,0},{9,1... | collective-permute-start | bytes 122888 | tf_op jit(solution)/shard_map/ppermute | solution.py:396
  54.7 5.2 %collective-permute-start.8 = (f32[2,5,8,128]{3,2,1,0:T(8,128)S(1)}, f32[2,5,8,128]{3,2,1,0:T(8,128)S(1)}, u32[]{:S(2)}, u32[]{:S(2)}) collective-permute-start(f32[2,5,8,128]{3,2,1,0:T(8,128)S(1)} %get-tuple-element.37.own), channel_id=1, source_target_pairs={{0,8},{1,9},{2,10},{3,11},{4,12},{5,13},{6,14},{7,15},{8,16},{9,17... | collective-permute-start | bytes 122888 | tf_op jit(solution)/shard_map/ppermute | solution.py:395
  56.1 4.0 %collective-permute-start.9 = (f32[2,5,8,128]{3,2,1,0:T(8,128)S(1)}, f32[2,5,8,128]{3,2,1,0:T(8,128)S(1)}, u32[]{:S(2)}, u32[]{:S(2)}) collective-permute-start(f32[2,5,8,128]{3,2,1,0:T(8,128)S(1)} %get-tuple-element.38), channel_id=1, source_target_pairs={{0,56},{1,57},{2,58},{3,59},{4,60},{5,61},{6,62},{7,63},{8,0},{9,1... | collective-permute-start | bytes 122888 | tf_op jit(solution)/shard_map/ppermute | solution.py:396
  83.0 1.3 %collective-permute-start.10 = (f32[64,128]{1,0:T(8,128)S(1)}, f32[64,128]{1,0:T(8,128)S(1)}, u32[]{:S(2)}, u32[]{:S(2)}) collective-permute-start(f32[64,128]{1,0:T(8,128)S(1)} %product.1), channel_id=1, source_target_pairs={{0,64},{64,0},{128,192},{192,128},{1,65},{65,1},{129,193},{193,129... | collective-permute-start | bytes 98312 | tf_op jit(solution)/shard_map/ppermute | solution.py:433
  84.3 3.7 %collective-permute-start.11 = (f32[16,128]{1,0:T(8,128)S(1)}, f32[16,128]{1,0:T(8,128)S(1)}, u32[]{:S(2)}, u32[]{:S(2)}) collective-permute-start(f32[16,128]{1,0:T(8,128)S(1)} %constant_dynamic-slice_fusion), channel_id=1, source_target_pairs={{0,128},{64,192},{128,0},{192,64},{1,129},{65,193},{129,1},{193,65... | collective-permute-start | bytes 24584 | tf_op jit(solution)/shard_map/ppermute | solution.py:436

commit v4 on v3

--- a/solution.py
+++ b/solution.py
@@ -333,7 +333,11 @@
     planes = group * depth
     everyone = bands * count
     in_plane = [[z * group + j for j in range(group)] for z in range(zs)]
-    along_z = [[z * group + j for z in range(zs)] for j in range(group)]
+    across = [
+        [b * grid + z * group + j for b in range(core, bands, 2) for z in range(zs)]
+        for core in range(2)
+        for j in range(group)
+    ]
     whole_plane = [[b * grid + z * group + j for b in range(bands) for j in range(group)] for z in range(zs)]
 
     parcel = call(
@@ -431,12 +435,15 @@
     )
     band = lax.axis_index("band")
     part = part + lax.ppermute(part, "band", [(i, i ^ 1) for i in range(bands)])
-    mine = lax.dynamic_slice_in_dim(part, band * count, count, axis=0)
-    other = lax.dynamic_slice_in_dim(part, (band ^ 2) * count, count, axis=0)
-    rows = mine + lax.ppermute(other, "band", [(i, i ^ 2) for i in range(bands)])
-
-    copies = jnp.broadcast_to(rows, (zs, *rows.shape))
-    copies = lax.all_to_all(copies, "grid", 0, 0, axis_index_groups=along_z, tiled=True)
+    core = band % 2
+    copies = jnp.concatenate(
+        [
+            jnp.broadcast_to(lax.dynamic_slice_in_dim(part, (2 * chip + core) * count, count, axis=0), (zs, count, nz))
+            for chip in range(bands // 2)
+        ],
+        axis=0,
+    )
+    copies = lax.all_to_all(copies, ("band", "grid"), 0, 0, axis_index_groups=across, tiled=True)
     packed = call(pack_kernel, "pack", shape((group, 18, ny, nz), f32), [VMEM, VMEM], VMEM)(current, copies)
     packed = lax.all_to_all(packed, "grid", 0, 0, axis_index_groups=in_plane, tiled=True)
     square = shape((count, everyone), f32)

time: 117 us -> 115 us (0.983)
  waiting for transfers between devices: 14.6 us -> 12.3 us
  blocking collectives: 48.3 us -> 49.9 us
    ppermute x1 -> x0, waiting for transfers between devices: 2.22 us -> none  [per_device(): lax.ppermute(other, 'band', [(i, i ^ 2) for i in range(bands)])]
    ppermute x1 -> x0, starting transfers between devices: 1.52 us -> none  [per_device(): lax.ppermute(other, 'band', [(i, i ^ 2) for i in range(bands)])]
  transfers between devices with their start and end apart: 13 -> 12, of which waited for: 11 -> 9; matrix products, arithmetic and copies ran while one was open for 1% -> 1% of each run, Pallas kernels for 11% -> 11%
where the time goes in v4:
time: 115 us; the launch traced here: 114 us
  blocking collectives  49.9 us (43%)
  starting transfers between devices  26.1 us (23%)
  Pallas kernels  24.1 us (21%)
  waiting for transfers between devices  12.3 us (11%)
    all_to_all x1, blocking collectives, per_device(): lax.all_to_all(send, ('band', 'grid'), 0, 0, axis_index_groups=whole_plan...  21.5 us
    all_to_all x1, blocking collectives, per_device(): lax.all_to_all(packed, 'grid', 0, 0, axis_index_groups=in_plane, tiled=True)  14.7 us
    all_to_all x1, blocking collectives, per_device(): lax.all_to_all(copies, ('band', 'grid'), 0, 0, axis_index_groups=across,...  13.8 us
    ppermute x5, starting transfers between devices, exchange(): lax.ppermute(down, 'grid', [(i, (i - group) % grid) for i in range(grid)])  11.9 us
    pallas_call x5, Pallas kernels, local(): call(functools.partial(stencil_kernel, mode), 'stencil', field, [VMEM] *...  8.46 us
    ppermute x5, starting transfers between devices, exchange(): lax.ppermute(up, 'grid', [(i, (i + group) % grid) for i in range(grid)])  8.04 us
    all_to_all x1, waiting for transfers between devices, per_device(): lax.all_to_all(parcel, 'grid', 0, 0, axis_index_groups=in_plane, tiled=True)  7.95 us
    all_to_all x1, starting transfers between devices, per_device(): lax.all_to_all(parcel, 'grid', 0, 0, axis_index_groups=in_plane, tiled=True)  6.04 us
  transfers between devices with their start and end apart: 12, of which 9 were waited for; matrix products, arithmetic and copies ran while one was open for 1% of the time, Pallas kernels for 11%

profile of v4, /device:TPU:2, one launch (start us, length us, event | category | flops | bytes accessed | tf_op | source)
XLA Modules:
  0.0 114.2 jit_solution(2333291680658922475)
XLA Ops:
  0.6 2.0 %parcel.1 = f32[8,3,8,8,128]{4,3,2,1,0:T(8,128)} custom-call(f32[8,2,8,8,128]{4,3,2,1,0:T(8,128)} %bitcast.15, f32[8,8,128]{2,1,0:T(8,128)} %potential.1), custom_call_target="tpu_custom_call" | custom-call | flops 4000000 | bytes 2000000 | tf_op jit(solution)/shard_map/parcel/pallas_call | solution.py:343
  2.6 6.0 %all-to-all-start = ((f32[8,3,8,8,128]{4,3,2,1,0:T(8,128)}), f32[8,3,8,8,128]{4,3,2,1,0:T(8,128)S(1)}, u32[]{:S(2)}, u32[]{:S(2)}) async-start(f32[8,3,8,8,128]{4,3,2,1,0:T(8,128)} %parcel.1), calls=%async_computation | async-start | bytes 1572864 | tf_op jit(solution)/shard_map/all_to_all | solution.py:355
  8.7 0.9 shift-right-arithmetic_reduce_fusion.1
  9.7 4.4 %build.1 = (f32[128,17,8,128]{3,2,1,0:T(8,128)}, s32[2,256]{1,0:T(2,128)S(4)}) custom-call(s32[2,128]{1,0:T(2,128)S(1)} %stack.4.info, s32[128,128]{1,0:T(8,128)} %idx_far.1, f32[128,128]{1,0:T(8,128)} %val_far.1), custom_call_target="tpu_custom_call" | custom-call | flops 4000000 | bytes 2000000 | tf_op jit(solution)/shard_map/build/pallas_call | solution.py:373
  14.1 7.9 %all-to-all-done.got.refs_0_.refs_1_ = f32[8,3,8,8,128]{4,3,2,1,0:T(8,128)S(1)} async-done(((f32[8,3,8,8,128]{4,3,2,1,0:T(8,128)}), f32[8,3,8,8,128]{4,3,2,1,0:T(8,128)S(1)}, u32[]{:S(2)}, u32[]{:S(2)}) %all-to-all-start) | async-done | bytes 786464 | tf_op jit(solution)/shard_map/all_to_all | solution.py:355
  22.1 2.0 %first.1 = (f32[2,64,8,128]{3,2,1,0:T(8,128)S(1)}, f32[2,5,8,128]{3,2,1,0:T(8,128)S(1)}, f32[2,5,8,128]{3,2,1,0:T(8,128)S(1)}, f32[128,17,8,128]{3,2,1,0:T(8,128)S(1)}) custom-call(s32[2,256]{1,0:T(2,128)S(4)} %get-tuple-element.21.table, f32[8,3,8,8,128]{4,3,2,1,0:T(8,128)S(1)} %all-to-all-done.got.refs_0_.refs_1_, ...), custom_call_target="tpu_custom_call" | custom-call | flops 4000000 | bytes 2000000 | tf_op jit(solution)/shard_map/first/pallas_call | solution.py:388
  24.1 2.1 %collective-permute-start = (f32[2,5,8,128]{3,2,1,0:T(8,128)S(1)}, f32[2,5,8,128]{3,2,1,0:T(8,128)S(1)}, u32[]{:S(2)}, u32[]{:S(2)}) collective-permute-start(f32[2,5,8,128]{3,2,1,0:T(8,128)S(1)} %get-tuple-element.25.own), channel_id=1, source_target_pairs={{0,8},{1,9},{2,10},{3,11},{4,12},{5,13},{6,14},{7,15},{8,16},{9,17... | collective-permute-start | bytes 122888 | tf_op jit(solution)/shard_map/ppermute | solution.py:399
  26.1 4.1 %collective-permute-start.1 = (f32[2,5,8,128]{3,2,1,0:T(8,128)S(1)}, f32[2,5,8,128]{3,2,1,0:T(8,128)S(1)}, u32[]{:S(2)}, u32[]{:S(2)}) collective-permute-start(f32[2,5,8,128]{3,2,1,0:T(8,128)S(1)} %get-tuple-element.26), channel_id=1, source_target_pairs={{0,56},{1,57},{2,58},{3,59},{4,60},{5,61},{6,62},{7,63},{8,0},{9,1... | collective-permute-start | bytes 122888 | tf_op jit(solution)/shard_map/ppermute | solution.py:400
  30.2 1.7 %stencil.5.partial = f32[2,64,8,128]{3,2,1,0:T(8,128)S(1)} custom-call(f32[2,64,8,128]{3,2,1,0:T(8,128)S(1)} %get-tuple-element.23.y.refs_0_, f32[8,3,8,8,128]{4,3,2,1,0:T(8,128)S(1)} %all-to-all-done.got.refs_0_.refs_1_), custom_call_target="tpu_custom_call" | custom-call | flops 4000000 | bytes 2000000 | tf_op jit(solution)/shard_map/stencil/pallas_call | solution.py:404
  32.1 1.1 finish.4
  33.2 3.6 %collective-permute-start.3 = (f32[2,5,8,128]{3,2,1,0:T(8,128)S(1)}, f32[2,5,8,128]{3,2,1,0:T(8,128)S(1)}, u32[]{:S(2)}, u32[]{:S(2)}) collective-permute-start(f32[2,5,8,128]{3,2,1,0:T(8,128)S(1)} %get-tuple-element.29), channel_id=1, source_target_pairs={{0,56},{1,57},{2,58},{3,59},{4,60},{5,61},{6,62},{7,63},{8,0},{9,1... | collective-permute-start | bytes 122888 | tf_op jit(solution)/shard_map/ppermute | solution.py:400
  36.8 1.7 %stencil.6.partial = f32[2,64,8,128]{3,2,1,0:T(8,128)S(1)} custom-call(f32[2,64,8,128]{3,2,1,0:T(8,128)S(1)} %get-tuple-element.27.y.refs_0_, f32[2,64,8,128]{3,2,1,0:T(8,128)S(1)} %get-tuple-element.23.y.refs_0_, f32[8,3,8,8,128]{4,3,2,1,0:T(8,128)S(1)} %all-to-all-done.got.refs_0_.refs_1_), custom_call_target="tpu_custom_call" | custom-call | flops 4000000 | bytes 2000000 | tf_op jit(solution)/shard_map/stencil/pallas_call | solution.py:404
  38.8 1.1 finish.5
  39.9 2.6 %collective-permute-start.4 = (f32[2,5,8,128]{3,2,1,0:T(8,128)S(1)}, f32[2,5,8,128]{3,2,1,0:T(8,128)S(1)}, u32[]{:S(2)}, u32[]{:S(2)}) collective-permute-start(f32[2,5,8,128]{3,2,1,0:T(8,128)S(1)} %get-tuple-element.31.own), channel_id=1, source_target_pairs={{0,8},{1,9},{2,10},{3,11},{4,12},{5,13},{6,14},{7,15},{8,16},{9,17... | collective-permute-start | bytes 122888 | tf_op jit(solution)/shard_map/ppermute | solution.py:399
  42.5 0.9 collective-permute-start.5
  43.5 1.7 %stencil.7.partial = f32[2,64,8,128]{3,2,1,0:T(8,128)S(1)} custom-call(f32[2,64,8,128]{3,2,1,0:T(8,128)S(1)} %get-tuple-element.30.y.refs_0_, f32[2,64,8,128]{3,2,1,0:T(8,128)S(1)} %get-tuple-element.27.y.refs_0_, f32[8,3,8,8,128]{4,3,2,1,0:T(8,128)S(1)} %all-to-all-done.got.refs_0_.refs_1_), custom_call_target="tpu_custom_call" | custom-call | flops 4000000 | bytes 2000000 | tf_op jit(solution)/shard_map/stencil/pallas_call | solution.py:404
  45.6 0.9 collective-permute-done.5.above
  46.5 1.1 finish.6
  47.6 2.1 %collective-permute-start.6 = (f32[2,5,8,128]{3,2,1,0:T(8,128)S(1)}, f32[2,5,8,128]{3,2,1,0:T(8,128)S(1)}, u32[]{:S(2)}, u32[]{:S(2)}) collective-permute-start(f32[2,5,8,128]{3,2,1,0:T(8,128)S(1)} %get-tuple-element.34.own), channel_id=1, source_target_pairs={{0,8},{1,9},{2,10},{3,11},{4,12},{5,13},{6,14},{7,15},{8,16},{9,17... | collective-permute-start | bytes 122888 | tf_op jit(solution)/shard_map/ppermute | solution.py:399
  49.7 1.2 %collective-permute-start.7 = (f32[2,5,8,128]{3,2,1,0:T(8,128)S(1)}, f32[2,5,8,128]{3,2,1,0:T(8,128)S(1)}, u32[]{:S(2)}, u32[]{:S(2)}) collective-permute-start(f32[2,5,8,128]{3,2,1,0:T(8,128)S(1)} %get-tuple-element.35), channel_id=1, source_target_pairs={{0,56},{1,57},{2,58},{3,59},{4,60},{5,61},{6,62},{7,63},{8,0},{9,1... | collective-permute-start | bytes 122888 | tf_op jit(solution)/shard_map/ppermute | solution.py:400
  50.8 1.7 %stencil.8.partial = f32[2,64,8,128]{3,2,1,0:T(8,128)S(1)} custom-call(f32[2,64,8,128]{3,2,1,0:T(8,128)S(1)} %get-tuple-element.33.y, f32[2,64,8,128]{3,2,1,0:T(8,128)S(1)} %get-tuple-element.30.y.refs_0_, f32[8,3,8,8,128]{4,3,2,1,0:T(8,128)S(1)} %all-to-all-done.got.refs_0_.refs_1_), custom_call_target="tpu_custom_call" | custom-call | flops 4000000 | bytes 2000000 | tf_op jit(solution)/shard_map/stencil/pallas_call | solution.py:404
  52.8 0.9 collective-permute-done.7.above
  53.7 1.1 finish.7
  54.8 1.2 %collective-permute-start.8 = (f32[2,5,8,128]{3,2,1,0:T(8,128)S(1)}, f32[2,5,8,128]{3,2,1,0:T(8,128)S(1)}, u32[]{:S(2)}, u32[]{:S(2)}) collective-permute-start(f32[2,5,8,128]{3,2,1,0:T(8,128)S(1)} %get-tuple-element.37.own), channel_id=1, source_target_pairs={{0,8},{1,9},{2,10},{3,11},{4,12},{5,13},{6,14},{7,15},{8,16},{9,17... | collective-permute-start | bytes 122888 | tf_op jit(solution)/shard_map/ppermute | solution.py:399
  56.0 2.0 %collective-permute-start.9 = (f32[2,5,8,128]{3,2,1,0:T(8,128)S(1)}, f32[2,5,8,128]{3,2,1,0:T(8,128)S(1)}, u32[]{:S(2)}, u32[]{:S(2)}) collective-permute-start(f32[2,5,8,128]{3,2,1,0:T(8,128)S(1)} %get-tuple-element.38), channel_id=1, source_target_pairs={{0,56},{1,57},{2,58},{3,59},{4,60},{5,61},{6,62},{7,63},{8,0},{9,1... | collective-permute-start | bytes 122888 | tf_op jit(solution)/shard_map/ppermute | solution.py:400
  58.0 1.7 %stencil.9.partial = f32[2,64,8,128]{3,2,1,0:T(8,128)S(1)} custom-call(f32[2,64,8,128]{3,2,1,0:T(8,128)S(1)} %get-tuple-element.36.y.refs_0_, f32[8,3,8,8,128]{4,3,2,1,0:T(8,128)S(1)} %all-to-all-done.got.refs_0_.refs_1_), custom_call_target="tpu_custom_call" | custom-call | flops 4000000 | bytes 2000000 | tf_op jit(solution)/shard_map/stencil/pallas_call | solution.py:404
  60.5 21.5 %all_to_all.20 = f32[32,2,2,16,128]{4,3,2,1,0:T(8,128)S(1)} all-to-all(f32[32,2,2,16,128]{4,3,2,1,0:T(8,128)S(1)} %image.1), channel_id=1, replica_groups={{0,1,2,3,4,5,6,7,64,65,66,67,68,69,70,71,128,129,130,131,132,133,134,13..., dimensions={0} | all-to-all | bytes 2097152 | tf_op jit(solution)/shard_map/all_to_all | solution.py:432
  82.0 1.5 %product.1 = f32[64,128]{1,0:T(8,128)S(1)} custom-call(f32[2048,128]{1,0:T(8,128)S(1)} %bitcast.9), custom_call_target="tpu_custom_call" | custom-call | flops 4000000 | bytes 2000000 | tf_op jit(solution)/shard_map/product/pallas_call | solution.py:433
  83.7 1.2 %collective-permute-done.10 = f32[64,128]{1,0:T(8,128)S(1)} collective-permute-done((f32[64,128]{1,0:T(8,128)S(1)}, f32[64,128]{1,0:T(8,128)S(1)}, u32[]{:S(2)}, u32[]{:S(2)}) %collective-permute-start.10) | collective-permute-done | bytes 32800 | tf_op jit(solution)/shard_map/ppermute | solution.py:437
  84.9 13.8 %all_to_all.21.parts = f32[16,16,128]{2,1,0:T(8,128)S(1)} all-to-all(f32[16,16,128]{2,1,0:T(8,128)S(1)} %pad_maximum_fusion), channel_id=1, replica_groups={{0,8,16,24,32,40,48,56,128,136,144,152,160,168,176,184},{1,9,17,25,33,4..., dimensions={0} | all-to-all | bytes 262144 | tf_op jit(solution)/shard_map/all_to_all | solution.py:446
  98.7 14.7 %all_to_all.22.got = f32[8,18,8,128]{3,2,1,0:T(8,128)S(1)} all-to-all(f32[8,18,8,128]{3,2,1,0:T(8,128)S(1)} %pack.1), channel_id=1, replica_groups={{0,1,2,3,4,5,6,7},{8,9,10,11,12,13,14,15},{16,17,18,19,20,21,22,23},{24..., dimensions={0} | all-to-all | bytes 1179648 | tf_op jit(solution)/shard_map/all_to_all | solution.py:448
  113.4 0.8 unpack.1
  (21 shorter events, 2.2 us)
Async XLA Ops:
  0.6 31.5 %copy-start = (f32[128]{0:T(128)S(1)}, f32[128]{0:T(128)}, u32[]{:S(2)}) copy-start(f32[128]{0:T(128)} %param.9) | copy-start | bytes 1540
  2.6 19.4 %all-to-all-start = ((f32[8,3,8,8,128]{4,3,2,1,0:T(8,128)}), f32[8,3,8,8,128]{4,3,2,1,0:T(8,128)S(1)}, u32[]{:S(2)}, u32[]{:S(2)}) async-start(f32[8,3,8,8,128]{4,3,2,1,0:T(8,128)} %parcel.1), calls=%async_computation | async-start | bytes 1572864 | tf_op jit(solution)/shard_map/all_to_all | solution.py:355
  24.1 8.1 %collective-permute-start = (f32[2,5,8,128]{3,2,1,0:T(8,128)S(1)}, f32[2,5,8,128]{3,2,1,0:T(8,128)S(1)}, u32[]{:S(2)}, u32[]{:S(2)}) collective-permute-start(f32[2,5,8,128]{3,2,1,0:T(8,128)S(1)} %get-tuple-element.25.own), channel_id=1, source_target_pairs={{0,8},{1,9},{2,10},{3,11},{4,12},{5,13},{6,14},{7,15},{8,16},{9,17... | collective-permute-start | bytes 122888 | tf_op jit(solution)/shard_map/ppermute | solution.py:399
  26.1 6.0 %collective-permute-start.1 = (f32[2,5,8,128]{3,2,1,0:T(8,128)S(1)}, f32[2,5,8,128]{3,2,1,0:T(8,128)S(1)}, u32[]{:S(2)}, u32[]{:S(2)}) collective-permute-start(f32[2,5,8,128]{3,2,1,0:T(8,128)S(1)} %get-tuple-element.26), channel_id=1, source_target_pairs={{0,56},{1,57},{2,58},{3,59},{4,60},{5,61},{6,62},{7,63},{8,0},{9,1... | collective-permute-start | bytes 122888 | tf_op jit(solution)/shard_map/ppermute | solution.py:400
  33.2 5.6 %collective-permute-start.2 = (f32[2,5,8,128]{3,2,1,0:T(8,128)S(1)}, f32[2,5,8,128]{3,2,1,0:T(8,128)S(1)}, u32[]{:S(2)}, u32[]{:S(2)}) collective-permute-start(f32[2,5,8,128]{3,2,1,0:T(8,128)S(1)} %get-tuple-element.28.own), channel_id=1, source_target_pairs={{0,8},{1,9},{2,10},{3,11},{4,12},{5,13},{6,14},{7,15},{8,16},{9,17... | collective-permute-start | bytes 122888 | tf_op jit(solution)/shard_map/ppermute | solution.py:399
  33.2 5.6 %collective-permute-start.3 = (f32[2,5,8,128]{3,2,1,0:T(8,128)S(1)}, f32[2,5,8,128]{3,2,1,0:T(8,128)S(1)}, u32[]{:S(2)}, u32[]{:S(2)}) collective-permute-start(f32[2,5,8,128]{3,2,1,0:T(8,128)S(1)} %get-tuple-element.29), channel_id=1, source_target_pairs={{0,56},{1,57},{2,58},{3,59},{4,60},{5,61},{6,62},{7,63},{8,0},{9,1... | collective-permute-start | bytes 122888 | tf_op jit(solution)/shard_map/ppermute | solution.py:400
  39.9 5.7 %collective-permute-start.4 = (f32[2,5,8,128]{3,2,1,0:T(8,128)S(1)}, f32[2,5,8,128]{3,2,1,0:T(8,128)S(1)}, u32[]{:S(2)}, u32[]{:S(2)}) collective-permute-start(f32[2,5,8,128]{3,2,1,0:T(8,128)S(1)} %get-tuple-element.31.own), channel_id=1, source_target_pairs={{0,8},{1,9},{2,10},{3,11},{4,12},{5,13},{6,14},{7,15},{8,16},{9,17... | collective-permute-start | bytes 122888 | tf_op jit(solution)/shard_map/ppermute | solution.py:399
  42.5 4.0 %collective-permute-start.5 = (f32[2,5,8,128]{3,2,1,0:T(8,128)S(1)}, f32[2,5,8,128]{3,2,1,0:T(8,128)S(1)}, u32[]{:S(2)}, u32[]{:S(2)}) collective-permute-start(f32[2,5,8,128]{3,2,1,0:T(8,128)S(1)} %get-tuple-element.32), channel_id=1, source_target_pairs={{0,56},{1,57},{2,58},{3,59},{4,60},{5,61},{6,62},{7,63},{8,0},{9,1... | collective-permute-start | bytes 122888 | tf_op jit(solution)/shard_map/ppermute | solution.py:400
  47.6 5.2 %collective-permute-start.6 = (f32[2,5,8,128]{3,2,1,0:T(8,128)S(1)}, f32[2,5,8,128]{3,2,1,0:T(8,128)S(1)}, u32[]{:S(2)}, u32[]{:S(2)}) collective-permute-start(f32[2,5,8,128]{3,2,1,0:T(8,128)S(1)} %get-tuple-element.34.own), channel_id=1, source_target_pairs={{0,8},{1,9},{2,10},{3,11},{4,12},{5,13},{6,14},{7,15},{8,16},{9,17... | collective-permute-start | bytes 122888 | tf_op jit(solution)/shard_map/ppermute | solution.py:399
  49.7 4.0 %collective-permute-start.7 = (f32[2,5,8,128]{3,2,1,0:T(8,128)S(1)}, f32[2,5,8,128]{3,2,1,0:T(8,128)S(1)}, u32[]{:S(2)}, u32[]{:S(2)}) collective-permute-start(f32[2,5,8,128]{3,2,1,0:T(8,128)S(1)} %get-tuple-element.35), channel_id=1, source_target_pairs={{0,56},{1,57},{2,58},{3,59},{4,60},{5,61},{6,62},{7,63},{8,0},{9,1... | collective-permute-start | bytes 122888 | tf_op jit(solution)/shard_map/ppermute | solution.py:400
  54.8 5.2 %collective-permute-start.8 = (f32[2,5,8,128]{3,2,1,0:T(8,128)S(1)}, f32[2,5,8,128]{3,2,1,0:T(8,128)S(1)}, u32[]{:S(2)}, u32[]{:S(2)}) collective-permute-start(f32[2,5,8,128]{3,2,1,0:T(8,128)S(1)} %get-tuple-element.37.own), channel_id=1, source_target_pairs={{0,8},{1,9},{2,10},{3,11},{4,12},{5,13},{6,14},{7,15},{8,16},{9,17... | collective-permute-start | bytes 122888 | tf_op jit(solution)/shard_map/ppermute | solution.py:399
  56.0 4.0 %collective-permute-start.9 = (f32[2,5,8,128]{3,2,1,0:T(8,128)S(1)}, f32[2,5,8,128]{3,2,1,0:T(8,128)S(1)}, u32[]{:S(2)}, u32[]{:S(2)}) collective-permute-start(f32[2,5,8,128]{3,2,1,0:T(8,128)S(1)} %get-tuple-element.38), channel_id=1, source_target_pairs={{0,56},{1,57},{2,58},{3,59},{4,60},{5,61},{6,62},{7,63},{8,0},{9,1... | collective-permute-start | bytes 122888 | tf_op jit(solution)/shard_map/ppermute | solution.py:400
  83.5 1.3 %collective-permute-start.10 = (f32[64,128]{1,0:T(8,128)S(1)}, f32[64,128]{1,0:T(8,128)S(1)}, u32[]{:S(2)}, u32[]{:S(2)}) collective-permute-start(f32[64,128]{1,0:T(8,128)S(1)} %product.1), channel_id=1, source_target_pairs={{0,64},{64,0},{128,192},{192,128},{1,65},{65,1},{129,193},{193,129... | collective-permute-start | bytes 98312 | tf_op jit(solution)/shard_map/ppermute | solution.py:437
